TPU v7x, 32 devices: a whole 2x2x4 slice. The times are simulated.
32 devices in a mesh: gx: 8 (over y, x, core), gy: 4 (over z).
Axes of the slice: x: 2, y: 2, z: 4, core: 2. Of those that a mesh axis runs over, the one named last changes fastest.
Arguments:
- populations: float32 [19, 32, 128, 128], P(None, 'gx', 'gy'), may hold values from 0.02 to 0.09
- marker_weights: bfloat16 [1536, 64, 128], P(('gx', 'gy')), may hold values from 0 to 0.03125
- marker_force: bfloat16 [1536, 3, 128], P(('gx', 'gy')), may hold values from -0.59765625 to 0.59765625
- owner_device: int32 [1536, 1], P(('gx', 'gy')), may hold values from 0 to 31; in each aligned block of 48 rows (0 to 47, 48 to 95, ...) at most 3 rows name the same one
- stencil_base: int32 [1536, 3], P(('gx', 'gy')), may hold values from 0 to 124, as said below
- block_swimmer: int32 [1536], P(('gx', 'gy')), may hold values from 0 to 127, as said below
Outputs:
- new_populations: float32 [19, 32, 128, 128], P(None, 'gx', 'gy')
- marker_velocity: float32 [1536, 3, 128], P(('gx', 'gy'))
- swimmer_velocity: float32 [3, 128], P(None, ('gx', 'gy'))
Inputs may be any that keep to these rules, and one draw needn't show every extreme that they name: `owner_device`: among the blocks held by one device (aligned runs of 48 rows), no device is named more than 3 times, and some device is named exactly 3 times. `stencil_base`: component 0 lies in 0 to 0, component 1 in 0 to 28, component 2 in 0 to 124; each bound is taken by some block. `block_swimmer`: the blocks held by device d (gx slowest) belong to swimmers d * 4 to d * 4 + 3, and every swimmer has a block.
All inputs are finite; a program needn't handle non-finite values.
Results may differ from a plain program's by a relative error of at most 0.00056.
Values may be sent and summed in bfloat16 or wider, within the bound.
No kernel may reach another device: no remote copies, remote signals or barrier semaphores. Data moves between devices by JAX's collectives and lax.ppermute only.
A program may use at most 64 MiB of HBM per device.

v0:
```python
import functools

import jax
import jax.numpy as jnp
import numpy as np
from jax import lax
from jax.experimental import pallas as pl
from jax.experimental.pallas import tpu as pltpu
from jax.sharding import PartitionSpec as P


STEN = 4
SWIM_DEV = 4
LANES = 128
SUB = 8
GROUP = STEN * STEN
CODE_LANE = 64
REST_LANE = 48
DUP_LANE = 96
WIDE_DUPS = 4
STEP = 4

velocities = np.array(
    [
        [0, 0, 0],
        [1, 0, 0],
        [-1, 0, 0],
        [0, 1, 0],
        [0, -1, 0],
        [0, 0, 1],
        [0, 0, -1],
        [1, 1, 0],
        [-1, -1, 0],
        [1, -1, 0],
        [-1, 1, 0],
        [1, 0, 1],
        [-1, 0, -1],
        [1, 0, -1],
        [-1, 0, 1],
        [0, 1, 1],
        [0, -1, -1],
        [0, 1, -1],
        [0, -1, 1],
    ]
)
opposite = [0, 2, 1, 4, 3, 6, 5, 8, 7, 10, 9, 12, 11, 14, 13, 16, 15, 18, 17]
lattice_weights = [1.0 / 3.0] + [1.0 / 18.0] * 6 + [1.0 / 36.0] * 12
relax_time = 0.8
speed_scale = 20.0
going_east = [1, 7, 9, 11, 13]
going_west = [2, 8, 10, 12, 14]


def lane_iota(rows=SUB):
    return lax.broadcasted_iota(jnp.int32, (rows, LANES), 1)


def sub_iota(rows=SUB):
    return lax.broadcasted_iota(jnp.int32, (rows, LANES), 0)


def swapped(first, second, axis, periodic):
    size = lax.axis_size(axis)
    inner = [(i, i ^ 1) for i in range(size)]
    outer = []
    for i in range(size):
        j = i + 1 if i % 2 == 1 else i - 1
        if periodic:
            outer.append((i, j % size))
        elif 0 <= j < size:
            outer.append((i, j))
    second = lax.ppermute(second, axis, outer)
    first = lax.ppermute(first, axis, inner)
    return first, second


def patch_kernel(
    capacity,
    strips,
    owner_far,
    base_far,
    weights_far,
    force_far,
    populations,
    send,
    rim_a,
    rim_b,
    owner,
    base,
    weights,
    force,
    bottom,
    top,
    rows,
    spread,
    patches,
    record,
    count,
    place,
    again,
    sems,
):
    held = weights.shape[0]
    cells = weights.shape[1]
    strip_cells = populations.shape[2]
    pieces = sems.shape[0] - 5
    part_blocks = held // pieces
    force_copy = pltpu.make_async_copy(force_far, force, sems.at[pieces])
    force_copy.start()
    copies = [
        pltpu.make_async_copy(
            weights_far.at[part_blocks * n : part_blocks * (n + 1)],
            weights.at[part_blocks * n : part_blocks * (n + 1)],
            sems.at[n],
        )
        for n in range(pieces)
    ]
    copies.append(pltpu.make_async_copy(owner_far, owner, sems.at[pieces + 1]))
    copies.append(pltpu.make_async_copy(base_far, base, sems.at[pieces + 2]))
    edge_copies = [
        pltpu.make_async_copy(populations.at[:, :, 0:SUB, :], bottom, sems.at[pieces + 3]),
        pltpu.make_async_copy(
            populations.at[:, :, strip_cells - SUB : strip_cells, :], top, sems.at[pieces + 4]
        ),
    ]
    for copy in copies + edge_copies:
        copy.start()
    targets = send.shape[0]
    lane, sub = lane_iota(16), sub_iota(16)

    def clear(i, _):
        record[i] = jnp.zeros((16, LANES), jnp.float32)
        return 0

    lax.fori_loop(0, targets, clear, 0, unroll=16)

    def reset(i, _):
        count[i] = 0
        return 0

    lax.fori_loop(0, targets, reset, 0, unroll=16)
    for copy in copies[pieces:]:
        copy.wait()
    extra = jnp.int32(0)
    for b in range(held):
        target = owner[0, b]
        rank = count[target]
        count[target] = rank + 1
        place[b] = target * 4 + rank
        strip = lax.rem(target, strips)
        y = base[1, b]
        north = (y >= strip_cells - 5) & (strip < strips - 1)
        south = (y <= 1) & (strip > 0)
        again[extra] = b * 4 + rank
        extra = extra + jnp.where(north | south, 1, 0)
    force_copy.wait()
    for k in range(3):
        rows[k] = force[k].astype(jnp.float32)
    for b in range(held):
        for k in range(3):
            spread[16 * b + 4 * k : 16 * b + 4 * k + 4, :] = jnp.broadcast_to(
                rows[k, b : b + 1, :], (4, LANES)
            )
        spread[16 * b + 12 : 16 * b + 16, :] = jnp.zeros((4, LANES), jnp.float32)
    for g in range(held // 4):
        if 4 * g % part_blocks == 0:
            copies[4 * g // part_blocks].wait()
        out = lax.dot_general(
            spread[64 * g : 64 * g + 64, :].astype(jnp.bfloat16),
            weights[4 * g : 4 * g + 4].reshape(4 * cells, LANES),
            (((1,), (1,)), ((), ())),
            preferred_element_type=jnp.float32,
        )
        for j in range(4):
            half = j // 2
            part = out[16 * j : 16 * j + 16, LANES * half : LANES * half + LANES]
            part = jnp.where(lane // GROUP == 4 * (j % 2) + sub % 4, part, 0.0)
            part = part + pltpu.roll(part, 64, 1)
            part = part + pltpu.roll(part, 32, 1)
            part = part + pltpu.roll(part, 16, 1)
            patches[g * 4 + j] = part

    def labelled(tile, slot, frame_y, z):
        label = jnp.where(sub == 12, frame_y + SUB, z + 1).astype(jnp.float32)
        return jnp.where((lane == CODE_LANE + slot) & ((sub == 12) | (sub == 13)), label, tile)

    for b in range(held):
        target, rank = place[b] >> 2, place[b] & 3
        low = GROUP * rank
        inside = (lane >= low) & (lane < low + GROUP) & (sub < 12)
        tile = jnp.where(inside, patches[b], record[target])
        record[target] = labelled(tile, rank, base[1, b], base[2, b])

    def put_again(n, _):
        item = again[n]
        b, rank = item >> 2, item & 3
        y, z = base[1, b], base[2, b]
        to_south = y <= 1
        target = owner[0, b] + jnp.where(to_south, -1, 1)
        half = jnp.where(to_south, 0, 1)
        q = rank + jnp.where(to_south, capacity, 0)
        moved = pltpu.roll(patches[b], 8 * ((q + half) & 1), 1)
        wide = q < WIDE_DUPS
        low = jnp.where(wide, DUP_LANE + 8 * q, 2 * LANES)
        tile = jnp.where((lane >= low) & (lane < low + 8) & (sub < 12), moved, record[target])
        tile = labelled(
            tile, capacity + q, y + jnp.where(to_south, strip_cells, -strip_cells), z
        )
        if 2 * capacity > WIDE_DUPS:
            last = tile[12:16, :]
            lane4 = lane_iota(4)
            for k in range(3):
                low = jnp.where(wide, 2 * LANES, GROUP * k + 8 * (q - WIDE_DUPS))
                last = jnp.where(
                    (lane4 >= low) & (lane4 < low + 8), moved[4 * k : 4 * k + 4, :], last
                )
            tile = jnp.concatenate([tile[0:12, :], last], axis=0)
        record[target] = tile
        return 0

    lax.fori_loop(0, extra, put_again, 0)
    for copy in edge_copies:
        copy.wait()
    write_rims(bottom, top, rim_a, rim_b)
    rest_lanes = (lane >= REST_LANE) & (lane < 2 * REST_LANE) & (sub < 12)

    def finish(i, _):
        tile = record[i]
        rest = tile - tile.astype(jnp.bfloat16).astype(jnp.float32)
        tile = jnp.where(rest_lanes, pltpu.roll(rest, REST_LANE, 1), tile)
        send[i] = tile.astype(jnp.bfloat16)
        return 0

    lax.fori_loop(0, targets, finish, 0, unroll=8)


def fold_tables(toward):
    ahead = [i for i in range(19) if velocities[i, 1] == toward]
    plain = 4 if toward == 1 else 3
    to_east, to_west = (9, 8) if toward == 1 else (7, 10)
    near = [i for i in range(19) if i != to_west]
    far = ahead + [0, 1, 5, plain]
    return ahead, near, far, (plain, to_east, to_west)


def rim_message(near_row, far_row, toward):
    ahead, near, far, (plain, to_east, to_west) = fold_tables(toward)
    folded = {i: near_row[i] for i in near}
    folded[plain] = near_row[plain] + 2.0 * near_row[to_west]
    folded[to_east] = near_row[to_east] - near_row[to_west]
    message = [folded[i] for i in near]
    others = [i for i in range(19) if i not in ahead]
    total = [None, None, None]
    mass = None
    for i in others:
        mass = far_row[i] if mass is None else mass + far_row[i]
        for k in (0, 2):
            if velocities[i, k] != 0:
                term = far_row[i] if velocities[i, k] == 1 else -far_row[i]
                total[k] = term if total[k] is None else total[k] + term
        if velocities[i, 1] == -toward:
            total[1] = far_row[i] if total[1] is None else total[1] + far_row[i]
    rest = {0: mass - total[0] - total[1] - total[2], 1: total[0], 5: total[2], plain: total[1]}
    return message + [rest[i] if i in rest else far_row[i] for i in far]


def write_rims(bottom, top, rim_a, rim_b):
    even = lax.rem(lax.axis_index("gy"), 2) == 0

    def row(edge, n):
        return [edge[i, :, n, :] for i in range(19)]

    up = rim_message(row(top, SUB - 1), row(top, SUB - 2), 1)
    down = rim_message(row(bottom, 0), row(bottom, 1), -1)
    for n in range(len(up)):
        rim_a[n] = jnp.where(even, up[n], down[n])
        rim_b[n] = jnp.where(even, down[n], up[n])


def collided(fields, forcing):
    pair_sum, pair_diff = {}, {}
    for i in range(1, 19, 2):
        pair_sum[i] = fields[i] + fields[i + 1]
        pair_diff[i] = fields[i] - fields[i + 1]
    density = fields[0]
    for i in range(1, 19, 2):
        density = density + pair_sum[i]
    momentum = []
    for k in range(3):
        total = relax_time * forcing[k]
        for i in range(1, 19, 2):
            if velocities[i, k] == 1:
                total = total + pair_diff[i]
            elif velocities[i, k] == -1:
                total = total - pair_diff[i]
        momentum.append(total)
    inverse = 1.0 / density
    keep = 1.0 - 1.0 / relax_time
    squares = momentum[0] * momentum[0] + momentum[1] * momentum[1] + momentum[2] * momentum[2]
    level = density - 1.5 * inverse * squares
    curve = 4.5 * inverse
    result = [None] * 19
    result[0] = keep * fields[0] + (lattice_weights[0] / relax_time) * level
    for i in range(1, 19, 2):
        along = None
        for k in range(3):
            if velocities[i, k] == 1:
                along = momentum[k] if along is None else along + momentum[k]
            elif velocities[i, k] == -1:
                along = -momentum[k] if along is None else along - momentum[k]
        share = lattice_weights[i] / relax_time
        even = share * (level + curve * along * along)
        odd = (3.0 * share) * along
        result[i] = keep * fields[i] + (even + odd)
        result[i + 1] = keep * fields[i + 1] + (even - odd)
    return result


def keep_tile(relaxed, tiles, x, t, values):
    for i in range(19):
        if t < tiles:
            relaxed[i, x, SUB + SUB * t : 2 * SUB + SUB * t, :] = values[i]
        else:
            relaxed[i, x, 0:SUB, :] = values[i]
            relaxed[i, x, SUB + SUB * tiles : 2 * SUB + SUB * tiles, :] = values[i]


def write_faces(relaxed, slabs, tiles, face_a, face_b):
    even = lax.rem(lax.axis_index("gx"), 2) == 0
    for n in range(5):
        for t in range(tiles + 1):
            low = SUB + SUB * t
            east = relaxed[going_east[n], slabs - 1, low : low + SUB, :]
            west = relaxed[going_west[n], 0, low : low + SUB, :]
            face_a[n, SUB * t : SUB * t + SUB, :] = jnp.where(even, east, west)
            face_b[n, SUB * t : SUB * t + SUB, :] = jnp.where(even, west, east)


def unpack_faces(face_a, face_b, tiles, rim_west, rim_east):
    even = lax.rem(lax.axis_index("gx"), 2) == 0
    for n in range(5):
        for t in range(tiles + 1):
            a = face_a[n, SUB * t : SUB * t + SUB, :]
            b = face_b[n, SUB * t : SUB * t + SUB, :]
            west = jnp.where(even, b, a)
            east = jnp.where(even, a, b)
            low = SUB + SUB * t
            rim_west[n, low : low + SUB, :] = west
            rim_east[n, low : low + SUB, :] = east
            if t == tiles:
                rim_west[n, 0:SUB, :] = west
                rim_east[n, 0:SUB, :] = east


def streamed(relaxed, rim_west, rim_east, slabs, tiles, x, t, walls):
    lane, sub = lane_iota(), sub_iota()

    def rows(i, plane, low):
        if plane < 0:
            return rim_west[going_east.index(i), low : low + SUB, :]
        if plane >= slabs:
            return rim_east[going_west.index(i), low : low + SUB, :]
        return relaxed[i, plane, low : low + SUB, :]

    low = SUB + SUB * t if t < tiles else 0
    high = SUB + SUB * tiles
    result = []
    for i in range(19):
        ex, ey, ez = (int(v) for v in velocities[i])
        plane = x - ex
        if t < tiles or ey == 0:
            source = rows(i, plane, low - ey)
        elif ey == 1:
            source = jnp.where(
                sub >= 4, pltpu.roll(rows(i, plane, 0), 1, 0), rows(i, plane, high - 1)
            )
        else:
            source = jnp.where(
                sub >= 4, rows(i, plane, 1), pltpu.roll(rows(i, plane, high), SUB - 1, 0)
            )
        outside = None
        if ez == 1:
            source = pltpu.roll(source, 1, 1)
            outside = lane == 0
        elif ez == -1:
            source = pltpu.roll(source, LANES - 1, 1)
            outside = lane == LANES - 1
        wall = None
        if t == 0 and ey == 1:
            wall = (sub == 0) & walls[0]
        if t == tiles - 1 and ey == -1:
            wall = (sub == SUB - 1) & walls[1]
        if wall is not None:
            outside = wall if outside is None else outside | wall
        if outside is not None:
            source = jnp.where(outside, relaxed[opposite[i], x, low : low + SUB, :], source)
        result.append(source)
    return result


def wall_flags():
    strip = lax.axis_index("gy")
    return strip == 0, strip == lax.axis_size("gy") - 1


def first_kernel(
    capacity,
    got,
    populations,
    rim_a,
    rim_b,
    relaxed,
    face_a,
    face_b,
    forcing,
    items,
    codes,
    arrived,
    placed,
    rim,
    listing,
    spare,
    crowd,
    sem,
):
    slabs, strip_cells = populations.shape[1], populations.shape[2]
    tiles = strip_cells // SUB
    sources = got.shape[0]
    nowhere = SUB * LANES
    lane, sub = lane_iota(), sub_iota()
    arrived[pl.ds(sources * 16, 16), :] = jnp.zeros((16, LANES), jnp.float32)

    def gather(s, _):
        tile = got[s].astype(jnp.float32)
        upper, lower = tile[0:SUB, :], tile[SUB:16, :]
        own_lanes = lane < REST_LANE
        back = LANES - REST_LANE
        new_upper = jnp.where(own_lanes, upper + pltpu.roll(upper, back, 1), upper)
        new_lower = jnp.where(own_lanes, lower + pltpu.roll(lower, back, 1), lower)
        if 2 * capacity > WIDE_DUPS:
            here = (lane >= REST_LANE) & (lane < REST_LANE + GROUP)
            first_rows = pltpu.roll(lower, 4, 0)
            upper_dups = jnp.where(
                sub < 4,
                pltpu.roll(first_rows, REST_LANE, 1),
                pltpu.roll(lower, REST_LANE - GROUP, 1),
            )
            lower_dups = pltpu.roll(first_rows, REST_LANE - 2 * GROUP, 1)
            new_upper = jnp.where(here, upper_dups, new_upper)
            new_lower = jnp.where(here & (sub < 4), lower_dups, new_lower)
        at = pl.multiple_of(s * 16, 16)
        arrived[pl.ds(at, SUB), :] = new_upper
        arrived[pl.ds(at + SUB, SUB), :] = new_lower
        return 0

    lax.fori_loop(0, sources, gather, 0, unroll=8)
    first_dup = CODE_LANE + capacity
    for n in range(sources // SUB):
        row = arrived[pl.ds(SUB * n * 16 + 12, SUB, stride=16), :].astype(jnp.int32)
        column = arrived[pl.ds(SUB * n * 16 + 13, SUB, stride=16), :].astype(jnp.int32)
        code = row * LANES + column - 1
        source = sub + SUB * n
        is_dup = lane >= first_dup
        slot = jnp.where(is_dup, source * 8 + lane - first_dup, source * 4 + lane - CODE_LANE)
        item = jnp.where(code >= 0, slot * 8192 + code, -1)
        busy = jnp.where(is_dup & (lane < first_dup + 2 * capacity) & (code >= 0), 1.0, 0.0)
        busy = jnp.sum(busy, axis=1, keepdims=True)
        item = jnp.where(lane == LANES - 1, jnp.where(busy > 0.0, 1, 0), item)
        corner = pltpu.roll(jnp.maximum(code, nowhere), LANES - CODE_LANE, 1)
        items[SUB * n : SUB * n + SUB, :] = jnp.where(lane < capacity, corner, item)
    copy = pltpu.make_async_copy(items, codes, sem)
    copy.start()
    even = lax.rem(lax.axis_index("gy"), 2) == 0
    rim[...] = jnp.zeros_like(rim)
    for toward in (1, -1):
        _, near, far, _ = fold_tables(toward)
        for n, i in enumerate(near + far):
            a, b = rim_a[n], rim_b[n]
            value = jnp.where(even, b, a) if toward == 1 else jnp.where(even, a, b)
            if toward == 1:
                at = 7 if n < len(near) else 6
            else:
                at = 0 if n < len(near) else 1
            rim[i, :, at, :] = value
    placed[...] = jnp.zeros_like(placed)
    copy.wait()

    def note(s, carry):
        own, some = carry
        for r in range(capacity):
            item = codes[s, CODE_LANE + r]
            listing[own >> 7, own & 127] = item
            own = own + 1 + (item >> 31)
        crowd[some] = s
        return own, some + codes[s, LANES - 1]

    own_count, some = lax.fori_loop(0, sources, note, (jnp.int32(0), jnp.int32(0)), unroll=8)

    def note_dup(n, dup):
        s = crowd[n]
        for r in range(2 * capacity):
            item = codes[s, first_dup + r]
            spare[dup] = item
            dup = dup + 1 + (item >> 31)
        return dup

    dup_count = lax.fori_loop(0, some, note_dup, jnp.int32(0))
    for j in range(STEP - 1):
        at = own_count + j
        listing[at >> 7, at & 127] = sources * 4 * 8192 + nowhere

    def moved_rows(source, z, lanes_at, steps):
        inside = (lane >= z) & (lane < z + STEN)
        rows = {}
        for h in range(2):
            tile = arrived[pl.ds(pl.multiple_of(source * 16, 16) + SUB * h, SUB), :]
            for b in range(steps):
                shift = (z - lanes_at - STEN * b + 2 * LANES) & (LANES - 1)
                rows[b, h] = jnp.where(inside, pltpu.roll(tile, shift, 1), 0.0)
        return rows

    def add_rows(rows, y):
        at = {
            (b, h): pl.ds(pl.multiple_of((y + b) * 16 + SUB * h, SUB), SUB) for b, h in rows
        }
        old = {key: placed[at[key], :] for key in rows}
        for key in rows:
            placed[at[key], :] = old[key] + rows[key]

    def place_own(n, _):
        todo = []
        for j in range(STEP):
            at = STEP * n + j
            item = listing[at >> 7, at & 127]
            slot, code = item >> 13, item & 8191
            todo.append(
                (moved_rows(slot >> 2, code & (LANES - 1), GROUP * (slot & 3), 4), code >> 7)
            )
        for rows, y in todo:
            add_rows(rows, y)
        return 0

    lax.fori_loop(0, (own_count + STEP - 1) // STEP, place_own, 0)

    def place_dup(n, _):
        item = spare[n]
        slot, code = item >> 13, item & 8191
        q = slot & 7
        low = jnp.where(q < capacity, 2, 0)
        at = 8 * q + jnp.where(q < WIDE_DUPS, DUP_LANE, REST_LANE - 8 * WIDE_DUPS)
        rows = moved_rows(slot >> 3, code & (LANES - 1), at, 2)
        add_rows(rows, (code >> 7) + low)
        return 0

    lax.fori_loop(0, dup_count, place_dup, 0)
    for x in range(slabs):
        for t in range(tiles + 1):
            push = []
            for k in range(3):
                if t < tiles:
                    value = placed[pl.ds((SUB + SUB * t) * 16 + 4 * k + x, SUB, stride=16), :]
                else:
                    value = jnp.where(
                        sub >= 4,
                        placed[pl.ds(4 * k + x, SUB, stride=16), :],
                        placed[pl.ds((SUB + SUB * tiles) * 16 + 4 * k + x, SUB, stride=16), :],
                    )
                forcing[k, x, SUB * t : SUB * t + SUB, :] = value
                push.append(value)
            if t < tiles:
                fields = [populations[i, x, SUB * t : SUB * t + SUB, :] for i in range(19)]
            else:
                fields = [rim[i, x] for i in range(19)]
            keep_tile(relaxed, tiles, x, t, collided(fields, push))
    write_faces(relaxed, slabs, tiles, face_a, face_b)


def second_kernel(before, got_a, got_b, forcing, relaxed, face_a, face_b, rim_west, rim_east):
    slabs = before.shape[1]
    tiles = before.shape[2] // SUB - 2
    unpack_faces(got_a, got_b, tiles, rim_west, rim_east)
    walls = wall_flags()
    for x in range(slabs):
        for t in range(tiles + 1):
            fields = streamed(before, rim_west, rim_east, slabs, tiles, x, t, walls)
            push = [forcing[k, x, SUB * t : SUB * t + SUB, :] for k in range(3)]
            keep_tile(relaxed, tiles, x, t, collided(fields, push))
    write_faces(relaxed, slabs, tiles, face_a, face_b)


def third_kernel(
    capacity,
    items,
    before,
    got_a,
    got_b,
    forcing,
    populations_far,
    speeds,
    corners,
    populations,
    rim_west,
    rim_east,
    fluid,
    sems,
):
    slabs = before.shape[1]
    corner_copy = pltpu.make_async_copy(items, corners, sems.at[slabs])
    corner_copy.start()
    tiles = before.shape[2] // SUB - 2
    unpack_faces(got_a, got_b, tiles, rim_west, rim_east)
    walls = wall_flags()
    copies = []
    for x in range(slabs):
        for t in range(tiles):
            fields = streamed(before, rim_west, rim_east, slabs, tiles, x, t, walls)
            density = fields[0]
            for i in range(1, 19):
                density = density + fields[i]
            inverse = 1.0 / density
            for i in range(19):
                populations[i, x, SUB * t : SUB * t + SUB, :] = fields[i]
            for k in range(3):
                total = 0.5 * forcing[k, x, SUB * t : SUB * t + SUB, :]
                for i in range(19):
                    if velocities[i, k] == 1:
                        total = total + fields[i]
                    elif velocities[i, k] == -1:
                        total = total - fields[i]
                fluid[pl.ds(SUB * t * 16 + 4 * k + x, SUB, stride=16), :] = total * inverse
        copies.append(
            pltpu.make_async_copy(populations.at[:, x], populations_far.at[:, x], sems.at[x])
        )
        copies[x].start()
    lane = lane_iota()
    corner_copy.wait()

    def pick(s, _):
        corner = [corners[s, r] for r in range(capacity)]
        tile = jnp.zeros((SUB, LANES), jnp.float32)
        for h in range(2):
            for r in range(capacity):
                y, z = (corner[r] >> 7) - SUB, corner[r] & (LANES - 1)
                for b in range(4):
                    low = GROUP * (h * capacity + r) + STEN * b
                    row = pl.multiple_of((y + b) * 16 + SUB * h, SUB)
                    shift = (low - z + LANES) & (LANES - 1)
                    moved = pltpu.roll(fluid[pl.ds(row, SUB), :], shift, 1)
                    tile = jnp.where((lane >= low) & (lane < low + STEN), moved, tile)
        speeds[s] = tile.astype(jnp.bfloat16)
        return 0

    lax.fori_loop(0, speeds.shape[0], pick, 0, unroll=8)
    for copy in copies:
        copy.wait()


def marker_kernel(
    capacity, owner, swimmer, returned, weights, velocity, total, chosen, expanded, count
):
    held = weights.shape[0]
    cells = weights.shape[1]
    targets = returned.shape[0]
    lane, sub = lane_iota(16), sub_iota(16)
    sub8, lane8 = sub_iota(), lane_iota()

    def reset(i, _):
        count[i] = 0
        return 0

    lax.fori_loop(0, targets, reset, 0, unroll=16)
    for b in range(held):
        target = owner[0, b]
        rank = count[target]
        count[target] = rank + 1
        low = GROUP * rank
        tile = returned[target].astype(jnp.float32)
        first = jnp.where((lane8 >= low) & (lane8 < low + GROUP), tile, 0.0)
        low = low + GROUP * capacity
        second = jnp.where((lane8 >= low) & (lane8 < low + GROUP), tile, 0.0)
        chosen[16 * b : 16 * b + 16, :] = jnp.concatenate([first, second], axis=0).astype(
            jnp.bfloat16
        )
    across = lax.broadcasted_iota(jnp.int32, (LANES, LANES), 1)
    down = lax.broadcasted_iota(jnp.int32, (LANES, LANES), 0)
    repeat = jnp.where(across % GROUP == down % GROUP, 1.0, 0.0).astype(jnp.bfloat16)
    own_cells = (lane // GROUP) % 4 == sub % 4
    for g in range(held // SUB):
        wide = jnp.dot(
            chosen[LANES * g : LANES * g + LANES, :], repeat, preferred_element_type=jnp.float32
        )
        for j in range(SUB):
            expanded[LANES * g + 16 * j : LANES * g + 16 * j + 16, :] = jnp.where(
                own_cells, wide[16 * j : 16 * j + 16, :], 0.0
            )
    sums = {}
    for g in range(held // SUB):
        pieces = []
        for k in range(3):
            row = None
            for x in range(4):
                part = expanded[pl.ds(LANES * g + 4 * k + x, SUB, stride=16), :]
                row = part if row is None else row + part
            pieces.append(
                jnp.concatenate(
                    [
                        jnp.where(sub8 == 2 * pair + lane8 // 64, row, 0.0).astype(jnp.bfloat16)
                        for pair in range(4)
                    ],
                    axis=1,
                )
            )
        left = jnp.concatenate(pieces, axis=0)
        right = weights[SUB * g : SUB * g + SUB].reshape(SUB * cells, LANES)
        out = speed_scale * jnp.dot(left, right, preferred_element_type=jnp.float32)
        member = jnp.zeros((SUB, LANES), jnp.int32)
        for j in range(SUB):
            member = jnp.where(sub8 == j, lax.rem(swimmer[SUB * g + j], SWIM_DEV), member)
        for k in range(3):
            part = out[SUB * k : SUB * k + SUB, :]
            velocity[k, SUB * g : SUB * g + SUB, :] = part
            for s in range(SWIM_DEV):
                term = jnp.where(member == s, part, 0.0)
                sums[k, s] = term if g == 0 else sums[k, s] + term
    table = jnp.zeros((SUB, LANES), jnp.float32)
    for (k, s), value in sums.items():
        mean = jnp.sum(value) * (1.0 / LANES)
        table = jnp.where((sub8 == k) & (lane8 == s), mean, table)
    total[...] = table[0:3, 0:SWIM_DEV]


VM = pl.BlockSpec(memory_space=pltpu.VMEM)
SM = pl.BlockSpec(memory_space=pltpu.SMEM)
FAR = pl.BlockSpec(memory_space=pltpu.HBM)


def shaped(shape, dtype=jnp.float32):
    return jax.ShapeDtypeStruct(shape, dtype)


def step(populations, marker_weights, marker_force, owner_device, stencil_base, block_swimmer):
    slab_cells, strip_cells, height = populations.shape[1:]
    strips = lax.axis_size("gy")
    devices = lax.axis_size("gx") * strips
    held = marker_weights.shape[0]
    capacity = max(2, (2 * held + devices - 1) // devices)
    padded_rows = strip_cells + 2 * SUB
    packed_rows = strip_cells + SUB
    f32 = jnp.float32
    small = pltpu.CompilerParams(vmem_limit_bytes=12 * 1024 * 1024)

    owner = owner_device.T
    force = marker_force.transpose(1, 0, 2)
    edge = shaped((27, slab_cells, height))
    edge_rows = pltpu.VMEM((19, slab_cells, SUB, height), f32)
    sent, rim_a, rim_b = pl.pallas_call(
        functools.partial(patch_kernel, capacity, strips),
        out_shape=(shaped((devices, 16, LANES), jnp.bfloat16), edge, edge),
        in_specs=[FAR] * 5,
        out_specs=(VM, VM, VM),
        scratch_shapes=[
            pltpu.SMEM(owner.shape, jnp.int32),
            pltpu.SMEM((3, held), jnp.int32),
            pltpu.VMEM(marker_weights.shape, jnp.bfloat16),
            pltpu.VMEM(force.shape, jnp.bfloat16),
            edge_rows,
            edge_rows,
            pltpu.VMEM((3, held, LANES), f32),
            pltpu.VMEM((held * 16, LANES), f32),
            pltpu.VMEM((held, 16, LANES), f32),
            pltpu.VMEM((devices, 16, LANES), f32),
            pltpu.SMEM((devices,), jnp.int32),
            pltpu.SMEM((held,), jnp.int32),
            pltpu.SMEM((held + 1,), jnp.int32),
            pltpu.SemaphoreType.DMA((9,)),
        ],
        name="patches",
    )(owner, stencil_base.T, marker_weights, force, populations)
    got = lax.all_to_all(sent, ("gx", "gy"), split_axis=0, concat_axis=0, tiled=True)
    rim_a, rim_b = swapped(rim_a, rim_b, "gy", False)
    planes = shaped((19, slab_cells, padded_rows, height))
    face = shaped((5, packed_rows, height))
    push = shaped((3, slab_cells, packed_rows, height))
    rims = [pltpu.VMEM((5, padded_rows, height), f32)] * 2
    relaxed, face_a, face_b, forcing, items = pl.pallas_call(
        functools.partial(first_kernel, capacity),
        out_shape=(planes, face, face, push, shaped((devices, LANES), jnp.int32)),
        in_specs=[VM] * 4,
        out_specs=(VM, VM, VM, VM, VM),
        scratch_shapes=[
            pltpu.SMEM((devices, LANES), jnp.int32),
            pltpu.VMEM(((devices + 1) * 16, LANES), f32),
            pltpu.VMEM((padded_rows * 16, LANES), f32),
            pltpu.VMEM((19, slab_cells, SUB, LANES), f32),
            pltpu.SMEM((SUB, LANES), jnp.int32),
            pltpu.SMEM((devices * 2 * capacity + 1,), jnp.int32),
            pltpu.SMEM((devices + 1,), jnp.int32),
            pltpu.SemaphoreType.DMA,
        ],
        compiler_params=small,
        name="first",
    )(got, populations, rim_a, rim_b)
    got_a, got_b = swapped(face_a, face_b, "gx", True)
    relaxed, face_a, face_b = pl.pallas_call(
        second_kernel,
        out_shape=(planes, face, face),
        in_specs=[VM] * 4,
        out_specs=(VM, VM, VM),
        scratch_shapes=rims,
        compiler_params=small,
        name="second",
    )(relaxed, got_a, got_b, forcing)
    got_a, got_b = swapped(face_a, face_b, "gx", True)
    fields, speeds = pl.pallas_call(
        functools.partial(third_kernel, capacity),
        out_shape=(shaped(populations.shape), shaped((devices, SUB, LANES), jnp.bfloat16)),
        in_specs=[VM, VM, VM, VM, VM],
        out_specs=(FAR, VM),
        scratch_shapes=[
            pltpu.SMEM((devices, LANES), jnp.int32),
            pltpu.VMEM(populations.shape, f32),
        ]
        + rims
        + [
            pltpu.VMEM((strip_cells * 16, LANES), f32),
            pltpu.SemaphoreType.DMA((slab_cells + 1,)),
        ],
        compiler_params=small,
        name="third",
    )(items, relaxed, got_a, got_b, forcing)
    returned = lax.all_to_all(speeds, ("gx", "gy"), split_axis=0, concat_axis=0, tiled=True)
    marker_velocity, swimmer_velocity = pl.pallas_call(
        functools.partial(marker_kernel, capacity),
        out_shape=(shaped((3, held, LANES)), shaped((3, SWIM_DEV))),
        in_specs=[SM, SM, VM, VM],
        out_specs=(VM, VM),
        scratch_shapes=[
            pltpu.VMEM((held * 16, LANES), jnp.bfloat16),
            pltpu.VMEM((held * 16, LANES), f32),
            pltpu.SMEM((devices,), jnp.int32),
        ],
        compiler_params=small,
        name="markers",
    )(owner, block_swimmer, returned, marker_weights)
    return fields, marker_velocity.transpose(1, 0, 2), swimmer_velocity


def solution(mesh):
    in_specs = (
        P(None, "gx", "gy", None),
        P(("gx", "gy"), None, None),
        P(("gx", "gy"), None, None),
        P(("gx", "gy"), None),
        P(("gx", "gy"), None),
        P(("gx", "gy")),
    )
    out_specs = (P(None, "gx", "gy", None), P(("gx", "gy"), None, None), P(None, ("gx", "gy")))
    return jax.shard_map(step, mesh=mesh, in_specs=in_specs, out_specs=out_specs, check_vma=False)
```

profile of v0, /device:TPU:0, one launch (start us, length us, event | category | flops | bytes accessed | tf_op | source)
XLA Modules:
  0.0 52.5 jit_solution(10903780362961829019)
XLA Ops:
  0.6 0.0 copy-start
  0.6 4.6 %patches.1 = (bf16[32,16,128]{2,1,0:T(8,128)(2,1)}, f32[27,4,128]{2,1,0:T(4,128)}, f32[27,4,128]{2,1,0:T(4,128)}) custom-call(s32[1,48]{1,0:T(1,128)} %bitcast.4, s32[3,48]{1,0:T(4,128)} %bitcast.7, bf16[48,64,128]{2,1,0:T(8,128)(2,1)} %weights.1, bf16[3,48,128]{2,1,0:T(8,128)(2,1)} %bitcast.6, f32[19,4,32,128]{3,2,1,0:T(8,128)} %populations.3), custom_call_target="tpu_custom_call" | custom-call | tf_op jit(solution)/shard_map/patches/pallas_call | solution.py:756
  5.3 7.1 %all-to-all-start = ((bf16[32,16,128]{2,1,0:T(8,128)(2,1)}), bf16[32,16,128]{2,1,0:T(8,128)(2,1)S(1)}, u32[]{:S(2)}, u32[]{:S(2)}) async-start(bf16[32,16,128]{2,1,0:T(8,128)(2,1)} %get-tuple-element.18), calls=%async_computation | async-start | bytes 262144 | tf_op jit(solution)/shard_map/all_to_all | solution.py:779
  12.4 1.8 %collective-permute-start = (f32[27,4,128]{2,1,0:T(4,128)}, f32[27,4,128]{2,1,0:T(4,128)S(1)}, u32[]{:S(2)}, u32[]{:S(2)}) collective-permute-start(f32[27,4,128]{2,1,0:T(4,128)} %get-tuple-element.19), channel_id=1, source_target_pairs={{0,1},{1,0},{2,3},{3,2},{4,5},{5,4},{6,7},{7,6},{8,9},{9,8},{10,11... | collective-permute-start | bytes 165896 | tf_op jit(solution)/shard_map/ppermute | solution.py:73
  14.2 0.7 %collective-permute-start.1 = (f32[27,4,128]{2,1,0:T(4,128)}, f32[27,4,128]{2,1,0:T(4,128)S(1)}, u32[]{:S(2)}, u32[]{:S(2)}) collective-permute-start(f32[27,4,128]{2,1,0:T(4,128)} %get-tuple-element.20), channel_id=1, source_target_pairs={{1,2},{2,1},{5,6},{6,5},{9,10},{10,9},{13,14},{14,13},{17,18},{18,... | collective-permute-start | bytes 165896 | tf_op jit(solution)/shard_map/ppermute | solution.py:72
  14.9 3.2 %collective-permute-done.rim_a = f32[27,4,128]{2,1,0:T(4,128)S(1)} collective-permute-done((f32[27,4,128]{2,1,0:T(4,128)}, f32[27,4,128]{2,1,0:T(4,128)S(1)}, u32[]{:S(2)}, u32[]{:S(2)}) %collective-permute-start) | collective-permute-done | bytes 55328 | tf_op jit(solution)/shard_map/ppermute | solution.py:73
  18.1 0.0 collective-permute-done.1.rim_b
  18.1 2.9 %all-to-all-done.got = bf16[32,16,128]{2,1,0:T(8,128)(2,1)S(1)} async-done(((bf16[32,16,128]{2,1,0:T(8,128)(2,1)}), bf16[32,16,128]{2,1,0:T(8,128)(2,1)S(1)}, u32[]{:S(2)}, u32[]{:S(2)}) %all-to-all-start) | async-done | bytes 131104 | tf_op jit(solution)/shard_map/all_to_all | solution.py:779
  21.1 0.0 copy-done
  21.1 4.2 %first.1 = (f32[19,4,48,128]{3,2,1,0:T(8,128)S(1)}, f32[5,40,128]{2,1,0:T(8,128)S(1)}, f32[5,40,128]{2,1,0:T(8,128)S(1)}, f32[3,4,40,128]{3,2,1,0:T(8,128)S(1)}, s32[32,128]{1,0:T(8,128)S(1)}) custom-call(bf16[32,16,128]{2,1,0:T(8,128)(2,1)S(1)} %all-to-all-done.got, f32[19,4,32,128]{3,2,1,0:T(8,128)S(1)} %copy-done, ...), custom_call_target="tpu_custom_call" | custom-call | tf_op jit(solution)/shard_map/first/pallas_call | solution.py:785
  25.3 0.1 collective-permute-start.2
  25.4 1.0 %collective-permute-start.3 = (f32[5,40,128]{2,1,0:T(8,128)S(1)}, f32[5,40,128]{2,1,0:T(8,128)S(1)}, u32[]{:S(2)}, u32[]{:S(2)}) collective-permute-start(f32[5,40,128]{2,1,0:T(8,128)S(1)} %get-tuple-element.24), channel_id=1, source_target_pairs={{0,28},{4,8},{8,4},{12,16},{16,12},{20,24},{24,20},{28,0},{1,29},{... | collective-permute-start | bytes 307208 | tf_op jit(solution)/shard_map/ppermute | solution.py:72
  26.3 0.3 collective-permute-done.2.got_a
  26.7 4.6 %collective-permute-done.3.got_b = f32[5,40,128]{2,1,0:T(8,128)S(1)} collective-permute-done((f32[5,40,128]{2,1,0:T(8,128)S(1)}, f32[5,40,128]{2,1,0:T(8,128)S(1)}, u32[]{:S(2)}, u32[]{:S(2)}) %collective-permute-start.3) | collective-permute-done | bytes 102432 | tf_op jit(solution)/shard_map/ppermute | solution.py:72
  31.2 0.7 %second.1 = (f32[19,4,48,128]{3,2,1,0:T(8,128)S(1)}, f32[5,40,128]{2,1,0:T(8,128)S(1)}, f32[5,40,128]{2,1,0:T(8,128)S(1)}) custom-call(f32[19,4,48,128]{3,2,1,0:T(8,128)S(1)} %get-tuple-element.22.before, f32[5,40,128]{2,1,0:T(8,128)S(1)} %collective-permute-done.2.got_a, f32[5,40,128]{2,1,0:T(8,128)S(1)} %collective-permute-done.3.got_b, ...), custom_call_target="tpu_custom_call" | custom-call | tf_op jit(solution)/shard_map/second/pallas_call | solution.py:804
  31.9 0.1 collective-permute-start.4
  32.0 0.8 %collective-permute-start.5 = (f32[5,40,128]{2,1,0:T(8,128)S(1)}, f32[5,40,128]{2,1,0:T(8,128)S(1)}, u32[]{:S(2)}, u32[]{:S(2)}) collective-permute-start(f32[5,40,128]{2,1,0:T(8,128)S(1)} %get-tuple-element.28), channel_id=1, source_target_pairs={{0,28},{4,8},{8,4},{12,16},{16,12},{20,24},{24,20},{28,0},{1,29},{... | collective-permute-start | bytes 307208 | tf_op jit(solution)/shard_map/ppermute | solution.py:72
  32.8 0.5 collective-permute-done.4.got_a
  33.3 4.2 %collective-permute-done.5.got_b = f32[5,40,128]{2,1,0:T(8,128)S(1)} collective-permute-done((f32[5,40,128]{2,1,0:T(8,128)S(1)}, f32[5,40,128]{2,1,0:T(8,128)S(1)}, u32[]{:S(2)}, u32[]{:S(2)}) %collective-permute-start.5) | collective-permute-done | bytes 102432 | tf_op jit(solution)/shard_map/ppermute | solution.py:72
  37.5 2.0 %third.1 = (f32[19,4,32,128]{3,2,1,0:T(8,128)}, bf16[32,8,128]{2,1,0:T(8,128)(2,1)S(1)}) custom-call(s32[32,128]{1,0:T(8,128)S(1)} %get-tuple-element.21.items, f32[19,4,48,128]{3,2,1,0:T(8,128)S(1)} %get-tuple-element.26.before, f32[5,40,128]{2,1,0:T(8,128)S(1)} %collective-permute-done.4.got_a, f32[5,40,128]{2,1,0:T(8,128)S(1)} %collective-permute-done.5.got_b, ...), custom_call_target="tpu_custom_call" | custom-call | tf_op jit(solution)/shard_map/third/pallas_call | solution.py:814
  39.5 11.1 %all_to_all.10.returned = bf16[32,8,128]{2,1,0:T(8,128)(2,1)S(1)} all-to-all(bf16[32,8,128]{2,1,0:T(8,128)(2,1)S(1)} %get-tuple-element.30), channel_id=1, replica_groups=mesh['gx'=8,'gy'=4] {'gx','gy'}, dimensions={0} | all-to-all | bytes 131072 | tf_op jit(solution)/shard_map/all_to_all | solution.py:831
  50.6 0.0 copy-done.1
  50.6 0.0 copy-done.2
  50.6 1.9 %markers.1 = (f32[3,48,128]{2,1,0:T(8,128)}, f32[3,4]{1,0:T(4,128)}) custom-call(s32[1,48]{1,0:T(1,128)S(1)} %bitcast.5, s32[48]{0:T(128)S(1)} %copy-done.3, bf16[32,8,128]{2,1,0:T(8,128)(2,1)S(1)} %all_to_all.10.returned, bf16[48,64,128]{2,1,0:T(8,128)(2,1)S(1)} %copy-done.1), custom_call_target="tpu_custom_call" | custom-call | tf_op jit(solution)/shard_map/markers/pallas_call | solution.py:832
  (4 shorter events, 0.0 us)
Async XLA Ops:
  0.6 20.4 %copy-start = (f32[19,4,32,128]{3,2,1,0:T(8,128)S(1)}, f32[19,4,32,128]{3,2,1,0:T(8,128)}, u32[]{:S(2)}) copy-start(f32[19,4,32,128]{3,2,1,0:T(8,128)} %populations.3) | copy-start | bytes 3735556
  5.3 15.8 %all-to-all-start = ((bf16[32,16,128]{2,1,0:T(8,128)(2,1)}), bf16[32,16,128]{2,1,0:T(8,128)(2,1)S(1)}, u32[]{:S(2)}, u32[]{:S(2)}) async-start(bf16[32,16,128]{2,1,0:T(8,128)(2,1)} %get-tuple-element.18), calls=%async_computation | async-start | bytes 262144 | tf_op jit(solution)/shard_map/all_to_all | solution.py:779
  12.4 5.7 %collective-permute-start = (f32[27,4,128]{2,1,0:T(4,128)}, f32[27,4,128]{2,1,0:T(4,128)S(1)}, u32[]{:S(2)}, u32[]{:S(2)}) collective-permute-start(f32[27,4,128]{2,1,0:T(4,128)} %get-tuple-element.19), channel_id=1, source_target_pairs={{0,1},{1,0},{2,3},{3,2},{4,5},{5,4},{6,7},{7,6},{8,9},{9,8},{10,11... | collective-permute-start | bytes 165896 | tf_op jit(solution)/shard_map/ppermute | solution.py:73
  14.2 3.9 %collective-permute-start.1 = (f32[27,4,128]{2,1,0:T(4,128)}, f32[27,4,128]{2,1,0:T(4,128)S(1)}, u32[]{:S(2)}, u32[]{:S(2)}) collective-permute-start(f32[27,4,128]{2,1,0:T(4,128)} %get-tuple-element.20), channel_id=1, source_target_pairs={{1,2},{2,1},{5,6},{6,5},{9,10},{10,9},{13,14},{14,13},{17,18},{18,... | collective-permute-start | bytes 165896 | tf_op jit(solution)/shard_map/ppermute | solution.py:72
  25.3 1.4 %collective-permute-start.2 = (f32[5,40,128]{2,1,0:T(8,128)S(1)}, f32[5,40,128]{2,1,0:T(8,128)S(1)}, u32[]{:S(2)}, u32[]{:S(2)}) collective-permute-start(f32[5,40,128]{2,1,0:T(8,128)S(1)} %get-tuple-element.23), channel_id=1, source_target_pairs={{0,4},{4,0},{8,12},{12,8},{16,20},{20,16},{24,28},{28,24},{1,5},{5... | collective-permute-start | bytes 307208 | tf_op jit(solution)/shard_map/ppermute | solution.py:73
  25.4 5.8 %collective-permute-start.3 = (f32[5,40,128]{2,1,0:T(8,128)S(1)}, f32[5,40,128]{2,1,0:T(8,128)S(1)}, u32[]{:S(2)}, u32[]{:S(2)}) collective-permute-start(f32[5,40,128]{2,1,0:T(8,128)S(1)} %get-tuple-element.24), channel_id=1, source_target_pairs={{0,28},{4,8},{8,4},{12,16},{16,12},{20,24},{24,20},{28,0},{1,29},{... | collective-permute-start | bytes 307208 | tf_op jit(solution)/shard_map/ppermute | solution.py:72
  31.2 19.4 %copy-start.1 = (bf16[48,64,128]{2,1,0:T(8,128)(2,1)S(1)}, bf16[48,64,128]{2,1,0:T(8,128)(2,1)}, u32[]{:S(2)}) copy-start(bf16[48,64,128]{2,1,0:T(8,128)(2,1)} %weights.1) | copy-start | bytes 2359300
  31.2 19.4 %copy-start.2 = (s32[48,1]{0,1:T(1,128)S(1)}, s32[48,1]{0,1:T(1,128)}, u32[]{:S(2)}) copy-start(s32[48,1]{0,1:T(1,128)} %param.9) | copy-start | bytes 580
  31.2 19.4 %copy-start.3 = (s32[48]{0:T(128)S(1)}, s32[48]{0:T(128)}, u32[]{:S(2)}) copy-start(s32[48]{0:T(128)} %swimmer.1) | copy-start | bytes 580
  31.9 1.4 %collective-permute-start.4 = (f32[5,40,128]{2,1,0:T(8,128)S(1)}, f32[5,40,128]{2,1,0:T(8,128)S(1)}, u32[]{:S(2)}, u32[]{:S(2)}) collective-permute-start(f32[5,40,128]{2,1,0:T(8,128)S(1)} %get-tuple-element.27), channel_id=1, source_target_pairs={{0,4},{4,0},{8,12},{12,8},{16,20},{20,16},{24,28},{28,24},{1,5},{5... | collective-permute-start | bytes 307208 | tf_op jit(solution)/shard_map/ppermute | solution.py:73
  32.0 5.5 %collective-permute-start.5 = (f32[5,40,128]{2,1,0:T(8,128)S(1)}, f32[5,40,128]{2,1,0:T(8,128)S(1)}, u32[]{:S(2)}, u32[]{:S(2)}) collective-permute-start(f32[5,40,128]{2,1,0:T(8,128)S(1)} %get-tuple-element.28), channel_id=1, source_target_pairs={{0,28},{4,8},{8,4},{12,16},{16,12},{20,24},{24,20},{28,0},{1,29},{... | collective-permute-start | bytes 307208 | tf_op jit(solution)/shard_map/ppermute | solution.py:72
where the time goes:
time: 52.7 us; the launch traced here: 52.5 us
  waiting for transfers between devices  15.8 us (30%)
  Pallas kernels  13.4 us (25%)
  starting transfers between devices  11.4 us (22%)
  blocking collectives  11.1 us (21%)
  between operations  0.71 us (1%)
    all_to_all x1, blocking collectives, step(): lax.all_to_all(speeds, ('gx', 'gy'), split_axis=0, concat_axis=0, tiled=T...  11.1 us
    ppermute x3, waiting for transfers between devices, swapped(): second = lax.ppermute(second, axis, outer)  8.78 us
    all_to_all x1, starting transfers between devices, step(): lax.all_to_all(sent, ('gx', 'gy'), split_axis=0, concat_axis=0, tiled=True)  7.09 us
    pallas_call x1, Pallas kernels, step(): pl.pallas_call(functools.partial(patch_kernel, capacity, strips), out_sha...  4.65 us
    pallas_call x1, Pallas kernels, step(): pl.pallas_call(functools.partial(first_kernel, capacity), out_shape=(plan...  4.2 us
    ppermute x3, waiting for transfers between devices, swapped(): first = lax.ppermute(first, axis, inner)  4.09 us
    all_to_all x1, waiting for transfers between devices, step(): lax.all_to_all(sent, ('gx', 'gy'), split_axis=0, concat_axis=0, tiled=True)  2.95 us
    ppermute x3, starting transfers between devices, swapped(): second = lax.ppermute(second, axis, outer)  2.38 us
  transfers between devices with their start and end apart: 7, of which 6 were waited for; matrix products, arithmetic and copies ran while one was open for 0% of the time, Pallas kernels for 0%

commit v1 on v0

--- a/solution.py
+++ b/solution.py
@@ -48,7 +48,9 @@
 relax_time = 0.8
 speed_scale = 20.0
 going_east = [1, 7, 9, 11, 13]
-going_west = [2, 8, 10, 12, 14]
+going_west = [2, 10, 8, 12, 14]
+staying = [0, 3, 4, 5, 6, 15, 16, 17, 18]
+FACE_FIELDS = 14
 
 
 def lane_iota(rows=SUB):
@@ -325,34 +327,121 @@
             relaxed[i, x, SUB + SUB * tiles : 2 * SUB + SUB * tiles, :] = values[i]
 
 
-def write_faces(relaxed, slabs, tiles, face_a, face_b):
+def write_faces(relaxed, forcing, slabs, tiles, walls, face_a, face_b):
     even = lax.rem(lax.axis_index("gx"), 2) == 0
-    for n in range(5):
-        for t in range(tiles + 1):
-            low = SUB + SUB * t
-            east = relaxed[going_east[n], slabs - 1, low : low + SUB, :]
-            west = relaxed[going_west[n], 0, low : low + SUB, :]
-            face_a[n, SUB * t : SUB * t + SUB, :] = jnp.where(even, east, west)
-            face_b[n, SUB * t : SUB * t + SUB, :] = jnp.where(even, west, east)
+    for t in range(tiles + 1):
+        low = SUB + SUB * t
+        sides = []
+        for going, plane in ((going_east, slabs - 1), (going_west, 0)):
+            fields = streamed(relaxed, None, None, slabs, tiles, plane, t, walls, going + staying)
+            mass = None
+            for value in fields.values():
+                mass = value if mass is None else mass + value
+            message = [relaxed[i, plane, low : low + SUB, :] for i in going]
+            message += [fields[i] for i in going] + [mass]
+            for k in range(3):
+                total = relax_time * forcing[k, plane, SUB * t : SUB * t + SUB, :]
+                message.append(with_signs(total, fields, k))
+            sides.append(message)
+        for n in range(FACE_FIELDS):
+            east, west = sides[0][n], sides[1][n]
+            a, b = jnp.where(even, east, west), jnp.where(even, west, east)
+            if t < tiles:
+                at = SUB * (tiles * n + t)
+                face_a[at : at + SUB, :] = a
+                face_b[at : at + SUB, :] = b
+            else:
+                at = SUB * tiles * FACE_FIELDS + 2 * n
+                for j, row in enumerate(rim_sublanes(n)):
+                    face_a[at + j : at + j + 1, :] = a[row : row + 1, :]
+                    face_b[at + j : at + j + 1, :] = b[row : row + 1, :]
+
+
+def rim_sublanes(n):
+    along = int(velocities[going_east[n], 1]) if n < 5 else 0
+    return {0: (7, 0), 1: (6, 7), -1: (0, 1)}[along]
+
+
+def with_signs(total, fields, k):
+    for i, value in fields.items():
+        if velocities[i, k] == 1:
+            total = total + value
+        elif velocities[i, k] == -1:
+            total = total - value
+    return total
 
 
 def unpack_faces(face_a, face_b, tiles, rim_west, rim_east):
     even = lax.rem(lax.axis_index("gx"), 2) == 0
     for n in range(5):
-        for t in range(tiles + 1):
-            a = face_a[n, SUB * t : SUB * t + SUB, :]
-            b = face_b[n, SUB * t : SUB * t + SUB, :]
-            west = jnp.where(even, b, a)
-            east = jnp.where(even, a, b)
-            low = SUB + SUB * t
-            rim_west[n, low : low + SUB, :] = west
-            rim_east[n, low : low + SUB, :] = east
-            if t == tiles:
-                rim_west[n, 0:SUB, :] = west
-                rim_east[n, 0:SUB, :] = east
-
-
-def streamed(relaxed, rim_west, rim_east, slabs, tiles, x, t, walls):
+        for t in range(tiles):
+            at = SUB * (tiles * n + t)
+            a, b = face_a[at : at + SUB, :], face_b[at : at + SUB, :]
+            keep_rim(rim_west, n, tiles, t, jnp.where(even, b, a))
+            keep_rim(rim_east, n, tiles, t, jnp.where(even, a, b))
+        at = SUB * tiles * FACE_FIELDS + 2 * n
+        for j, row in enumerate(rim_sublanes(n)):
+            a, b = face_a[at + j : at + j + 1, :], face_b[at + j : at + j + 1, :]
+            places = [row] if row >= 4 else [row, SUB + SUB * tiles + row]
+            for place in places:
+                rim_west[n, place : place + 1, :] = jnp.where(even, b, a)
+                rim_east[n, place : place + 1, :] = jnp.where(even, a, b)
+
+
+def keep_rim(rim, n, tiles, t, value):
+    low = SUB + SUB * t
+    rim[n, low : low + SUB, :] = value
+    if t == tiles:
+        rim[n, 0:SUB, :] = value
+
+
+def relax_rim(
+    relaxed, rims, slabs, tiles, walls, face_a, face_b, going, back, plane, is_west, after
+):
+    even = lax.rem(lax.axis_index("gx"), 2) == 0
+    for t in range(tiles + 1):
+
+        def got(n):
+            at = SUB * (tiles * n + t) if t < tiles else SUB * tiles * FACE_FIELDS + 2 * n
+            size = SUB if t < tiles else 1
+            a, b = face_a[at : at + size, :], face_b[at : at + size, :]
+            value = jnp.where(even, b, a) if is_west else jnp.where(even, a, b)
+            if t < tiles:
+                return value
+            a, b = face_a[at + 1 : at + 2, :], face_b[at + 1 : at + 2, :]
+            last = jnp.where(even, b, a) if is_west else jnp.where(even, a, b)
+            return jnp.where(sub_iota() >= 4, value, last)
+
+        fields = streamed(relaxed, rims[0], rims[1], slabs, tiles, plane, t, walls, back)
+        density = got(10)
+        for value in fields.values():
+            density = density + value
+        momentum = [with_signs(got(11 + k), fields, k) for k in range(3)]
+        inward = {i: got(5 + n) for n, i in enumerate(going)}
+        for n, value in enumerate(collided_some(inward, density, momentum).values()):
+            keep_rim(after, n, tiles, t, value)
+
+
+def collided_some(fields, density, momentum):
+    inverse = 1.0 / density
+    keep = 1.0 - 1.0 / relax_time
+    squares = momentum[0] * momentum[0] + momentum[1] * momentum[1] + momentum[2] * momentum[2]
+    level = density - 1.5 * inverse * squares
+    curve = 4.5 * inverse
+    result = {}
+    for i, value in fields.items():
+        along = jnp.zeros_like(density)
+        for k in range(3):
+            if velocities[i, k] == 1:
+                along = along + momentum[k]
+            elif velocities[i, k] == -1:
+                along = along - momentum[k]
+        share = lattice_weights[i] / relax_time
+        result[i] = keep * value + (share * (level + curve * along * along) + (3.0 * share) * along)
+    return result
+
+
+def streamed(relaxed, rim_west, rim_east, slabs, tiles, x, t, walls, chosen=tuple(range(19))):
     lane, sub = lane_iota(), sub_iota()
 
     def rows(i, plane, low):
@@ -364,8 +453,8 @@
 
     low = SUB + SUB * t if t < tiles else 0
     high = SUB + SUB * tiles
-    result = []
-    for i in range(19):
+    result = {}
+    for i in chosen:
         ex, ey, ez = (int(v) for v in velocities[i])
         plane = x - ex
         if t < tiles or ey == 0:
@@ -393,8 +482,8 @@
         if wall is not None:
             outside = wall if outside is None else outside | wall
         if outside is not None:
-            source = jnp.where(outside, relaxed[opposite[i], x, low : low + SUB, :], source)
-        result.append(source)
+            source = jnp.where(outside, rows(opposite[i], x, low), source)
+        result[i] = source
     return result
 
 
@@ -572,23 +661,10 @@
             else:
                 fields = [rim[i, x] for i in range(19)]
             keep_tile(relaxed, tiles, x, t, collided(fields, push))
-    write_faces(relaxed, slabs, tiles, face_a, face_b)
-
-
-def second_kernel(before, got_a, got_b, forcing, relaxed, face_a, face_b, rim_west, rim_east):
-    slabs = before.shape[1]
-    tiles = before.shape[2] // SUB - 2
-    unpack_faces(got_a, got_b, tiles, rim_west, rim_east)
-    walls = wall_flags()
-    for x in range(slabs):
-        for t in range(tiles + 1):
-            fields = streamed(before, rim_west, rim_east, slabs, tiles, x, t, walls)
-            push = [forcing[k, x, SUB * t : SUB * t + SUB, :] for k in range(3)]
-            keep_tile(relaxed, tiles, x, t, collided(fields, push))
-    write_faces(relaxed, slabs, tiles, face_a, face_b)
-
-
-def third_kernel(
+    write_faces(relaxed, forcing, slabs, tiles, wall_flags(), face_a, face_b)
+
+
+def second_kernel(
     capacity,
     items,
     before,
@@ -599,8 +675,11 @@
     speeds,
     corners,
     populations,
+    relaxed,
     rim_west,
     rim_east,
+    after_west,
+    after_east,
     fluid,
     sems,
 ):
@@ -610,10 +689,33 @@
     tiles = before.shape[2] // SUB - 2
     unpack_faces(got_a, got_b, tiles, rim_west, rim_east)
     walls = wall_flags()
+    rims = (rim_west, rim_east)
+    relax_rim(
+        before, rims, slabs, tiles, walls, got_a, got_b, going_east, going_west, -1, True, after_west
+    )
+    relax_rim(
+        before,
+        rims,
+        slabs,
+        tiles,
+        walls,
+        got_a,
+        got_b,
+        going_west,
+        going_east,
+        slabs,
+        False,
+        after_east,
+    )
+    for x in range(slabs):
+        for t in range(tiles + 1):
+            fields = streamed(before, rim_west, rim_east, slabs, tiles, x, t, walls)
+            push = [forcing[k, x, SUB * t : SUB * t + SUB, :] for k in range(3)]
+            keep_tile(relaxed, tiles, x, t, collided(fields, push))
     copies = []
     for x in range(slabs):
         for t in range(tiles):
-            fields = streamed(before, rim_west, rim_east, slabs, tiles, x, t, walls)
+            fields = streamed(relaxed, after_west, after_east, slabs, tiles, x, t, walls)
             density = fields[0]
             for i in range(1, 19):
                 density = density + fields[i]
@@ -779,9 +881,9 @@
     got = lax.all_to_all(sent, ("gx", "gy"), split_axis=0, concat_axis=0, tiled=True)
     rim_a, rim_b = swapped(rim_a, rim_b, "gy", False)
     planes = shaped((19, slab_cells, padded_rows, height))
-    face = shaped((5, packed_rows, height))
+    face = shaped((FACE_FIELDS * strip_cells + 4 * SUB, height))
     push = shaped((3, slab_cells, packed_rows, height))
-    rims = [pltpu.VMEM((5, padded_rows, height), f32)] * 2
+    rims = [pltpu.VMEM((5, padded_rows, height), f32)] * 4
     relaxed, face_a, face_b, forcing, items = pl.pallas_call(
         functools.partial(first_kernel, capacity),
         out_shape=(planes, face, face, push, shaped((devices, LANES), jnp.int32)),
@@ -801,24 +903,15 @@
         name="first",
     )(got, populations, rim_a, rim_b)
     got_a, got_b = swapped(face_a, face_b, "gx", True)
-    relaxed, face_a, face_b = pl.pallas_call(
-        second_kernel,
-        out_shape=(planes, face, face),
-        in_specs=[VM] * 4,
-        out_specs=(VM, VM, VM),
-        scratch_shapes=rims,
-        compiler_params=small,
-        name="second",
-    )(relaxed, got_a, got_b, forcing)
-    got_a, got_b = swapped(face_a, face_b, "gx", True)
     fields, speeds = pl.pallas_call(
-        functools.partial(third_kernel, capacity),
+        functools.partial(second_kernel, capacity),
         out_shape=(shaped(populations.shape), shaped((devices, SUB, LANES), jnp.bfloat16)),
         in_specs=[VM, VM, VM, VM, VM],
         out_specs=(FAR, VM),
         scratch_shapes=[
             pltpu.SMEM((devices, LANES), jnp.int32),
             pltpu.VMEM(populations.shape, f32),
+            pltpu.VMEM(planes.shape, f32),
         ]
         + rims
         + [
@@ -826,7 +919,7 @@
             pltpu.SemaphoreType.DMA((slab_cells + 1,)),
         ],
         compiler_params=small,
-        name="third",
+        name="second",
     )(items, relaxed, got_a, got_b, forcing)
     returned = lax.all_to_all(speeds, ("gx", "gy"), split_axis=0, concat_axis=0, tiled=True)
     marker_velocity, swimmer_velocity = pl.pallas_call(

time: 52.7 us -> 50.3 us (0.954)
  waiting for transfers between devices: 15.8 us -> 14.1 us
  starting transfers between devices: 11.4 us -> 10.6 us
    ppermute x3 -> x2, waiting for transfers between devices: 8.78 us -> 7.42 us  [swapped(): second = lax.ppermute(second, axis, outer)]
    ppermute x3 -> x2, starting transfers between devices: 2.38 us -> 1.61 us  [swapped(): second = lax.ppermute(second, axis, outer)]
    ppermute x3 -> x2, waiting for transfers between devices: 4.09 us -> 3.77 us  [swapped(): first = lax.ppermute(first, axis, inner)]
    pallas_call x2 -> x1, Pallas kernels: 2.67 us -> 2.53 us  [step(): pl.pallas_call(functools.partial(second_kernel, capacity), out_shape=(sha...]
    ppermute x3 -> x2, starting transfers between devices: 1.98 us -> 1.91 us  [swapped(): first = lax.ppermute(first, axis, inner)]
  transfers between devices with their start and end apart: 7 -> 5, of which waited for: 6 -> 4; matrix products, arithmetic and copies ran while one was open for 0% -> 0% of each run, Pallas kernels for 0% -> 0%
where the time goes in v1:
time: 50.3 us; the launch traced here: 50 us
  waiting for transfers between devices  14.1 us (28%)
  Pallas kernels  13.4 us (27%)
  blocking collectives  11.2 us (22%)
  starting transfers between devices  10.6 us (21%)
  between operations  0.7 us (1%)
    all_to_all x1, blocking collectives, step(): lax.all_to_all(speeds, ('gx', 'gy'), split_axis=0, concat_axis=0, tiled=T...  11.2 us
    ppermute x2, waiting for transfers between devices, swapped(): second = lax.ppermute(second, axis, outer)  7.42 us
    all_to_all x1, starting transfers between devices, step(): lax.all_to_all(sent, ('gx', 'gy'), split_axis=0, concat_axis=0, tiled=True)  7.09 us
    pallas_call x1, Pallas kernels, step(): pl.pallas_call(functools.partial(patch_kernel, capacity, strips), out_sha...  4.65 us
    pallas_call x1, Pallas kernels, step(): pl.pallas_call(functools.partial(first_kernel, capacity), out_shape=(plan...  4.33 us
    ppermute x2, waiting for transfers between devices, swapped(): first = lax.ppermute(first, axis, inner)  3.77 us
    all_to_all x1, waiting for transfers between devices, step(): lax.all_to_all(sent, ('gx', 'gy'), split_axis=0, concat_axis=0, tiled=True)  2.95 us
    pallas_call x1, Pallas kernels, step(): pl.pallas_call(functools.partial(second_kernel, capacity), out_shape=(sha...  2.53 us
  transfers between devices with their start and end apart: 5, of which 4 were waited for; matrix products, arithmetic and copies ran while one was open for 0% of the time, Pallas kernels for 0%

profile of v1, /device:TPU:0, one launch (start us, length us, event | category | flops | bytes accessed | tf_op | source)
XLA Modules:
  0.0 50.0 jit_solution(17362678563442783403)
XLA Ops:
  0.6 0.0 copy-start
  0.6 4.6 %patches.1 = (bf16[32,16,128]{2,1,0:T(8,128)(2,1)}, f32[27,4,128]{2,1,0:T(4,128)}, f32[27,4,128]{2,1,0:T(4,128)}) custom-call(s32[1,48]{1,0:T(1,128)} %bitcast.4, s32[3,48]{1,0:T(4,128)} %bitcast.7, bf16[48,64,128]{2,1,0:T(8,128)(2,1)} %weights.1, bf16[3,48,128]{2,1,0:T(8,128)(2,1)} %bitcast.6, f32[19,4,32,128]{3,2,1,0:T(8,128)} %populations.3), custom_call_target="tpu_custom_call" | custom-call | tf_op jit(solution)/shard_map/patches/pallas_call | solution.py:858
  5.3 7.1 %all-to-all-start = ((bf16[32,16,128]{2,1,0:T(8,128)(2,1)}), bf16[32,16,128]{2,1,0:T(8,128)(2,1)S(1)}, u32[]{:S(2)}, u32[]{:S(2)}) async-start(bf16[32,16,128]{2,1,0:T(8,128)(2,1)} %get-tuple-element.15), calls=%async_computation | async-start | bytes 262144 | tf_op jit(solution)/shard_map/all_to_all | solution.py:881
  12.4 1.8 %collective-permute-start = (f32[27,4,128]{2,1,0:T(4,128)}, f32[27,4,128]{2,1,0:T(4,128)S(1)}, u32[]{:S(2)}, u32[]{:S(2)}) collective-permute-start(f32[27,4,128]{2,1,0:T(4,128)} %get-tuple-element.16), channel_id=1, source_target_pairs={{0,1},{1,0},{2,3},{3,2},{4,5},{5,4},{6,7},{7,6},{8,9},{9,8},{10,11... | collective-permute-start | bytes 165896 | tf_op jit(solution)/shard_map/ppermute | solution.py:75
  14.2 0.7 %collective-permute-start.1 = (f32[27,4,128]{2,1,0:T(4,128)}, f32[27,4,128]{2,1,0:T(4,128)S(1)}, u32[]{:S(2)}, u32[]{:S(2)}) collective-permute-start(f32[27,4,128]{2,1,0:T(4,128)} %get-tuple-element.17), channel_id=1, source_target_pairs={{1,2},{2,1},{5,6},{6,5},{9,10},{10,9},{13,14},{14,13},{17,18},{18,... | collective-permute-start | bytes 165896 | tf_op jit(solution)/shard_map/ppermute | solution.py:74
  14.9 3.2 %collective-permute-done.rim_a = f32[27,4,128]{2,1,0:T(4,128)S(1)} collective-permute-done((f32[27,4,128]{2,1,0:T(4,128)}, f32[27,4,128]{2,1,0:T(4,128)S(1)}, u32[]{:S(2)}, u32[]{:S(2)}) %collective-permute-start) | collective-permute-done | bytes 55328 | tf_op jit(solution)/shard_map/ppermute | solution.py:75
  18.1 0.0 collective-permute-done.1.rim_b
  18.1 2.9 %all-to-all-done.got = bf16[32,16,128]{2,1,0:T(8,128)(2,1)S(1)} async-done(((bf16[32,16,128]{2,1,0:T(8,128)(2,1)}), bf16[32,16,128]{2,1,0:T(8,128)(2,1)S(1)}, u32[]{:S(2)}, u32[]{:S(2)}) %all-to-all-start) | async-done | bytes 131104 | tf_op jit(solution)/shard_map/all_to_all | solution.py:881
  21.1 0.0 copy-done
  21.1 4.3 %first.1 = (f32[19,4,48,128]{3,2,1,0:T(8,128)S(1)}, f32[480,128]{1,0:T(8,128)S(1)}, f32[480,128]{1,0:T(8,128)S(1)}, f32[3,4,40,128]{3,2,1,0:T(8,128)S(1)}, s32[32,128]{1,0:T(8,128)S(1)}) custom-call(bf16[32,16,128]{2,1,0:T(8,128)(2,1)S(1)} %all-to-all-done.got, f32[19,4,32,128]{3,2,1,0:T(8,128)S(1)} %copy-done, ...), custom_call_target="tpu_custom_call" | custom-call | tf_op jit(solution)/shard_map/first/pallas_call | solution.py:887
  25.4 0.1 collective-permute-start.2
  25.5 1.0 %collective-permute-start.3 = (f32[480,128]{1,0:T(8,128)S(1)}, f32[480,128]{1,0:T(8,128)S(1)}, u32[]{:S(2)}, u32[]{:S(2)}) collective-permute-start(f32[480,128]{1,0:T(8,128)S(1)} %get-tuple-element.21), channel_id=1, source_target_pairs={{0,28},{4,8},{8,4},{12,16},{16,12},{20,24},{24,20},{28,0},{1,29},{... | collective-permute-start | bytes 737288 | tf_op jit(solution)/shard_map/ppermute | solution.py:74
  26.4 0.5 %collective-permute-done.2.got_a = f32[480,128]{1,0:T(8,128)S(1)} collective-permute-done((f32[480,128]{1,0:T(8,128)S(1)}, f32[480,128]{1,0:T(8,128)S(1)}, u32[]{:S(2)}, u32[]{:S(2)}) %collective-permute-start.2) | collective-permute-done | bytes 245792 | tf_op jit(solution)/shard_map/ppermute | solution.py:75
  27.0 7.4 %collective-permute-done.3.got_b = f32[480,128]{1,0:T(8,128)S(1)} collective-permute-done((f32[480,128]{1,0:T(8,128)S(1)}, f32[480,128]{1,0:T(8,128)S(1)}, u32[]{:S(2)}, u32[]{:S(2)}) %collective-permute-start.3) | collective-permute-done | bytes 245792 | tf_op jit(solution)/shard_map/ppermute | solution.py:74
  34.4 0.0 copy-start.1
  34.4 0.0 copy-start.2
  34.4 0.0 copy-start.3
  34.4 2.5 %second.1 = (f32[19,4,32,128]{3,2,1,0:T(8,128)}, bf16[32,8,128]{2,1,0:T(8,128)(2,1)S(1)}) custom-call(s32[32,128]{1,0:T(8,128)S(1)} %get-tuple-element.18.items, f32[19,4,48,128]{3,2,1,0:T(8,128)S(1)} %get-tuple-element.19.before, f32[480,128]{1,0:T(8,128)S(1)} %collective-permute-done.2.got_a, f32[480,128]{1,0:T(8,128)S(1)} %collective-permute-done.3.got_b, ...), custom_call_target="tpu_custom_call" | custom-call | tf_op jit(solution)/shard_map/second/pallas_call | solution.py:906
  36.9 11.2 %all_to_all.10.returned = bf16[32,8,128]{2,1,0:T(8,128)(2,1)S(1)} all-to-all(bf16[32,8,128]{2,1,0:T(8,128)(2,1)S(1)} %get-tuple-element.24), channel_id=1, replica_groups=mesh['gx'=8,'gy'=4] {'gx','gy'}, dimensions={0} | all-to-all | bytes 131072 | tf_op jit(solution)/shard_map/all_to_all | solution.py:924
  48.2 0.0 copy-done.1
  48.2 0.0 copy-done.2
  48.2 0.0 copy-done.3
  48.2 1.9 %markers.1 = (f32[3,48,128]{2,1,0:T(8,128)}, f32[3,4]{1,0:T(4,128)}) custom-call(s32[1,48]{1,0:T(1,128)S(1)} %bitcast.5, s32[48]{0:T(128)S(1)} %copy-done.3, bf16[32,8,128]{2,1,0:T(8,128)(2,1)S(1)} %all_to_all.10.returned, bf16[48,64,128]{2,1,0:T(8,128)(2,1)S(1)} %copy-done.1), custom_call_target="tpu_custom_call" | custom-call | tf_op jit(solution)/shard_map/markers/pallas_call | solution.py:925
Async XLA Ops:
  0.6 20.4 %copy-start = (f32[19,4,32,128]{3,2,1,0:T(8,128)S(1)}, f32[19,4,32,128]{3,2,1,0:T(8,128)}, u32[]{:S(2)}) copy-start(f32[19,4,32,128]{3,2,1,0:T(8,128)} %populations.3) | copy-start | bytes 3735556
  5.3 15.8 %all-to-all-start = ((bf16[32,16,128]{2,1,0:T(8,128)(2,1)}), bf16[32,16,128]{2,1,0:T(8,128)(2,1)S(1)}, u32[]{:S(2)}, u32[]{:S(2)}) async-start(bf16[32,16,128]{2,1,0:T(8,128)(2,1)} %get-tuple-element.15), calls=%async_computation | async-start | bytes 262144 | tf_op jit(solution)/shard_map/all_to_all | solution.py:881
  12.4 5.7 %collective-permute-start = (f32[27,4,128]{2,1,0:T(4,128)}, f32[27,4,128]{2,1,0:T(4,128)S(1)}, u32[]{:S(2)}, u32[]{:S(2)}) collective-permute-start(f32[27,4,128]{2,1,0:T(4,128)} %get-tuple-element.16), channel_id=1, source_target_pairs={{0,1},{1,0},{2,3},{3,2},{4,5},{5,4},{6,7},{7,6},{8,9},{9,8},{10,11... | collective-permute-start | bytes 165896 | tf_op jit(solution)/shard_map/ppermute | solution.py:75
  14.2 3.9 %collective-permute-start.1 = (f32[27,4,128]{2,1,0:T(4,128)}, f32[27,4,128]{2,1,0:T(4,128)S(1)}, u32[]{:S(2)}, u32[]{:S(2)}) collective-permute-start(f32[27,4,128]{2,1,0:T(4,128)} %get-tuple-element.17), channel_id=1, source_target_pairs={{1,2},{2,1},{5,6},{6,5},{9,10},{10,9},{13,14},{14,13},{17,18},{18,... | collective-permute-start | bytes 165896 | tf_op jit(solution)/shard_map/ppermute | solution.py:74
  25.4 1.6 %collective-permute-start.2 = (f32[480,128]{1,0:T(8,128)S(1)}, f32[480,128]{1,0:T(8,128)S(1)}, u32[]{:S(2)}, u32[]{:S(2)}) collective-permute-start(f32[480,128]{1,0:T(8,128)S(1)} %get-tuple-element.20), channel_id=1, source_target_pairs={{0,4},{4,0},{8,12},{12,8},{16,20},{20,16},{24,28},{28,24},{1,5},{5... | collective-permute-start | bytes 737288 | tf_op jit(solution)/shard_map/ppermute | solution.py:75
  25.5 8.9 %collective-permute-start.3 = (f32[480,128]{1,0:T(8,128)S(1)}, f32[480,128]{1,0:T(8,128)S(1)}, u32[]{:S(2)}, u32[]{:S(2)}) collective-permute-start(f32[480,128]{1,0:T(8,128)S(1)} %get-tuple-element.21), channel_id=1, source_target_pairs={{0,28},{4,8},{8,4},{12,16},{16,12},{20,24},{24,20},{28,0},{1,29},{... | collective-permute-start | bytes 737288 | tf_op jit(solution)/shard_map/ppermute | solution.py:74
  34.4 13.8 %copy-start.1 = (bf16[48,64,128]{2,1,0:T(8,128)(2,1)S(1)}, bf16[48,64,128]{2,1,0:T(8,128)(2,1)}, u32[]{:S(2)}) copy-start(bf16[48,64,128]{2,1,0:T(8,128)(2,1)} %weights.1) | copy-start | bytes 2359300
  34.4 13.8 %copy-start.2 = (s32[48,1]{0,1:T(1,128)S(1)}, s32[48,1]{0,1:T(1,128)}, u32[]{:S(2)}) copy-start(s32[48,1]{0,1:T(1,128)} %param.9) | copy-start | bytes 580
  34.4 13.8 %copy-start.3 = (s32[48]{0:T(128)S(1)}, s32[48]{0:T(128)}, u32[]{:S(2)}) copy-start(s32[48]{0:T(128)} %swimmer.1) | copy-start | bytes 580

commit v2 on v1

--- a/solution.py
+++ b/solution.py
@@ -492,32 +492,31 @@
     return strip == 0, strip == lax.axis_size("gy") - 1
 
 
-def first_kernel(
-    capacity,
-    got,
-    populations,
-    rim_a,
-    rim_b,
-    relaxed,
-    face_a,
-    face_b,
-    forcing,
-    items,
-    codes,
-    arrived,
-    placed,
-    rim,
-    listing,
-    spare,
-    crowd,
-    sem,
+def place_kernel(
+    capacity, got, placed, items, codes, arrived, listing, spare, crowd, sem
 ):
-    slabs, strip_cells = populations.shape[1], populations.shape[2]
-    tiles = strip_cells // SUB
     sources = got.shape[0]
     nowhere = SUB * LANES
     lane, sub = lane_iota(), sub_iota()
     arrived[pl.ds(sources * 16, 16), :] = jnp.zeros((16, LANES), jnp.float32)
+    for s in range(sources):
+        arrived[16 * s + SUB : 16 * s + 16, :] = got[s].astype(jnp.float32)[SUB:16, :]
+    first_dup = CODE_LANE + capacity
+    for n in range(sources // SUB):
+        row = arrived[pl.ds(SUB * n * 16 + 12, SUB, stride=16), :].astype(jnp.int32)
+        column = arrived[pl.ds(SUB * n * 16 + 13, SUB, stride=16), :].astype(jnp.int32)
+        code = row * LANES + column - 1
+        source = sub + SUB * n
+        is_dup = lane >= first_dup
+        slot = jnp.where(is_dup, source * 8 + lane - first_dup, source * 4 + lane - CODE_LANE)
+        item = jnp.where(code >= 0, slot * 8192 + code, -1)
+        busy = jnp.where(is_dup & (lane < first_dup + 2 * capacity) & (code >= 0), 1.0, 0.0)
+        busy = jnp.sum(busy, axis=1, keepdims=True)
+        item = jnp.where(lane == LANES - 1, jnp.where(busy > 0.0, 1, 0), item)
+        corner = pltpu.roll(jnp.maximum(code, nowhere), LANES - CODE_LANE, 1)
+        items[SUB * n : SUB * n + SUB, :] = jnp.where(lane < capacity, corner, item)
+    copy = pltpu.make_async_copy(items, codes, sem)
+    copy.start()
 
     def gather(s, _):
         tile = got[s].astype(jnp.float32)
@@ -543,22 +542,83 @@
         return 0
 
     lax.fori_loop(0, sources, gather, 0, unroll=8)
-    first_dup = CODE_LANE + capacity
-    for n in range(sources // SUB):
-        row = arrived[pl.ds(SUB * n * 16 + 12, SUB, stride=16), :].astype(jnp.int32)
-        column = arrived[pl.ds(SUB * n * 16 + 13, SUB, stride=16), :].astype(jnp.int32)
-        code = row * LANES + column - 1
-        source = sub + SUB * n
-        is_dup = lane >= first_dup
-        slot = jnp.where(is_dup, source * 8 + lane - first_dup, source * 4 + lane - CODE_LANE)
-        item = jnp.where(code >= 0, slot * 8192 + code, -1)
-        busy = jnp.where(is_dup & (lane < first_dup + 2 * capacity) & (code >= 0), 1.0, 0.0)
-        busy = jnp.sum(busy, axis=1, keepdims=True)
-        item = jnp.where(lane == LANES - 1, jnp.where(busy > 0.0, 1, 0), item)
-        corner = pltpu.roll(jnp.maximum(code, nowhere), LANES - CODE_LANE, 1)
-        items[SUB * n : SUB * n + SUB, :] = jnp.where(lane < capacity, corner, item)
-    copy = pltpu.make_async_copy(items, codes, sem)
-    copy.start()
+    placed[...] = jnp.zeros_like(placed)
+    copy.wait()
+
+    def note(s, carry):
+        own, some = carry
+        for r in range(capacity):
+            item = codes[s, CODE_LANE + r]
+            listing[own >> 7, own & 127] = item
+            own = own + 1 + (item >> 31)
+        crowd[some] = s
+        return own, some + codes[s, LANES - 1]
+
+    own_count, some = lax.fori_loop(0, sources, note, (jnp.int32(0), jnp.int32(0)), unroll=8)
+
+    def note_dup(n, dup):
+        s = crowd[n]
+        for r in range(2 * capacity):
+            item = codes[s, first_dup + r]
+            spare[dup] = item
+            dup = dup + 1 + (item >> 31)
+        return dup
+
+    dup_count = lax.fori_loop(0, some, note_dup, jnp.int32(0))
+    for j in range(STEP - 1):
+        at = own_count + j
+        listing[at >> 7, at & 127] = sources * 4 * 8192 + nowhere
+
+    def moved_rows(source, z, lanes_at, steps):
+        inside = (lane >= z) & (lane < z + STEN)
+        rows = {}
+        for h in range(2):
+            tile = arrived[pl.ds(pl.multiple_of(source * 16, 16) + SUB * h, SUB), :]
+            for b in range(steps):
+                shift = (z - lanes_at - STEN * b + 2 * LANES) & (LANES - 1)
+                rows[b, h] = jnp.where(inside, pltpu.roll(tile, shift, 1), 0.0)
+        return rows
+
+    def add_rows(rows, y):
+        at = {
+            (b, h): pl.ds(pl.multiple_of((y + b) * 16 + SUB * h, SUB), SUB) for b, h in rows
+        }
+        old = {key: placed[at[key], :] for key in rows}
+        for key in rows:
+            placed[at[key], :] = old[key] + rows[key]
+
+    def place_own(n, _):
+        todo = []
+        for j in range(STEP):
+            at = STEP * n + j
+            item = listing[at >> 7, at & 127]
+            slot, code = item >> 13, item & 8191
+            todo.append(
+                (moved_rows(slot >> 2, code & (LANES - 1), GROUP * (slot & 3), 4), code >> 7)
+            )
+        for rows, y in todo:
+            add_rows(rows, y)
+        return 0
+
+    lax.fori_loop(0, (own_count + STEP - 1) // STEP, place_own, 0)
+
+    def place_dup(n, _):
+        item = spare[n]
+        slot, code = item >> 13, item & 8191
+        q = slot & 7
+        low = jnp.where(q < capacity, 2, 0)
+        at = 8 * q + jnp.where(q < WIDE_DUPS, DUP_LANE, REST_LANE - 8 * WIDE_DUPS)
+        rows = moved_rows(slot >> 3, code & (LANES - 1), at, 2)
+        add_rows(rows, (code >> 7) + low)
+        return 0
+
+    lax.fori_loop(0, dup_count, place_dup, 0)
+
+
+def first_kernel(placed, populations, rim_a, rim_b, relaxed, face_a, face_b, forcing, rim):
+    slabs, strip_cells = populations.shape[1], populations.shape[2]
+    tiles = strip_cells // SUB
+    sub = sub_iota()
     even = lax.rem(lax.axis_index("gy"), 2) == 0
     rim[...] = jnp.zeros_like(rim)
     for toward in (1, -1):
@@ -571,77 +631,6 @@
             else:
                 at = 0 if n < len(near) else 1
             rim[i, :, at, :] = value
-    placed[...] = jnp.zeros_like(placed)
-    copy.wait()
-
-    def note(s, carry):
-        own, some = carry
-        for r in range(capacity):
-            item = codes[s, CODE_LANE + r]
-            listing[own >> 7, own & 127] = item
-            own = own + 1 + (item >> 31)
-        crowd[some] = s
-        return own, some + codes[s, LANES - 1]
-
-    own_count, some = lax.fori_loop(0, sources, note, (jnp.int32(0), jnp.int32(0)), unroll=8)
-
-    def note_dup(n, dup):
-        s = crowd[n]
-        for r in range(2 * capacity):
-            item = codes[s, first_dup + r]
-            spare[dup] = item
-            dup = dup + 1 + (item >> 31)
-        return dup
-
-    dup_count = lax.fori_loop(0, some, note_dup, jnp.int32(0))
-    for j in range(STEP - 1):
-        at = own_count + j
-        listing[at >> 7, at & 127] = sources * 4 * 8192 + nowhere
-
-    def moved_rows(source, z, lanes_at, steps):
-        inside = (lane >= z) & (lane < z + STEN)
-        rows = {}
-        for h in range(2):
-            tile = arrived[pl.ds(pl.multiple_of(source * 16, 16) + SUB * h, SUB), :]
-            for b in range(steps):
-                shift = (z - lanes_at - STEN * b + 2 * LANES) & (LANES - 1)
-                rows[b, h] = jnp.where(inside, pltpu.roll(tile, shift, 1), 0.0)
-        return rows
-
-    def add_rows(rows, y):
-        at = {
-            (b, h): pl.ds(pl.multiple_of((y + b) * 16 + SUB * h, SUB), SUB) for b, h in rows
-        }
-        old = {key: placed[at[key], :] for key in rows}
-        for key in rows:
-            placed[at[key], :] = old[key] + rows[key]
-
-    def place_own(n, _):
-        todo = []
-        for j in range(STEP):
-            at = STEP * n + j
-            item = listing[at >> 7, at & 127]
-            slot, code = item >> 13, item & 8191
-            todo.append(
-                (moved_rows(slot >> 2, code & (LANES - 1), GROUP * (slot & 3), 4), code >> 7)
-            )
-        for rows, y in todo:
-            add_rows(rows, y)
-        return 0
-
-    lax.fori_loop(0, (own_count + STEP - 1) // STEP, place_own, 0)
-
-    def place_dup(n, _):
-        item = spare[n]
-        slot, code = item >> 13, item & 8191
-        q = slot & 7
-        low = jnp.where(q < capacity, 2, 0)
-        at = 8 * q + jnp.where(q < WIDE_DUPS, DUP_LANE, REST_LANE - 8 * WIDE_DUPS)
-        rows = moved_rows(slot >> 3, code & (LANES - 1), at, 2)
-        add_rows(rows, (code >> 7) + low)
-        return 0
-
-    lax.fori_loop(0, dup_count, place_dup, 0)
     for x in range(slabs):
         for t in range(tiles + 1):
             push = []
@@ -884,24 +873,31 @@
     face = shaped((FACE_FIELDS * strip_cells + 4 * SUB, height))
     push = shaped((3, slab_cells, packed_rows, height))
     rims = [pltpu.VMEM((5, padded_rows, height), f32)] * 4
-    relaxed, face_a, face_b, forcing, items = pl.pallas_call(
-        functools.partial(first_kernel, capacity),
-        out_shape=(planes, face, face, push, shaped((devices, LANES), jnp.int32)),
-        in_specs=[VM] * 4,
-        out_specs=(VM, VM, VM, VM, VM),
+    placed, items = pl.pallas_call(
+        functools.partial(place_kernel, capacity),
+        out_shape=(shaped((padded_rows * 16, LANES)), shaped((devices, LANES), jnp.int32)),
+        in_specs=[VM],
+        out_specs=(VM, VM),
         scratch_shapes=[
             pltpu.SMEM((devices, LANES), jnp.int32),
             pltpu.VMEM(((devices + 1) * 16, LANES), f32),
-            pltpu.VMEM((padded_rows * 16, LANES), f32),
-            pltpu.VMEM((19, slab_cells, SUB, LANES), f32),
             pltpu.SMEM((SUB, LANES), jnp.int32),
             pltpu.SMEM((devices * 2 * capacity + 1,), jnp.int32),
             pltpu.SMEM((devices + 1,), jnp.int32),
             pltpu.SemaphoreType.DMA,
         ],
         compiler_params=small,
+        name="place",
+    )(got)
+    relaxed, face_a, face_b, forcing = pl.pallas_call(
+        first_kernel,
+        out_shape=(planes, face, face, push),
+        in_specs=[VM] * 4,
+        out_specs=(VM, VM, VM, VM),
+        scratch_shapes=[pltpu.VMEM((19, slab_cells, SUB, LANES), f32)],
+        compiler_params=small,
         name="first",
-    )(got, populations, rim_a, rim_b)
+    )(placed, populations, rim_a, rim_b)
     got_a, got_b = swapped(face_a, face_b, "gx", True)
     fields, speeds = pl.pallas_call(
         functools.partial(second_kernel, capacity),

time: 50.3 us -> 48.1 us (0.956)
  blocking collectives: 11.2 us -> 9.19 us
    all_to_all x1, waiting for transfers between devices: 2.95 us -> 6.18 us  [step(): lax.all_to_all(sent, ('gx', 'gy'), split_axis=0, concat_axis=0, tiled=True)]
    ppermute x2, waiting for transfers between devices: 3.77 us -> 0.54 us  [swapped(): first = lax.ppermute(first, axis, inner)]
    all_to_all x1, blocking collectives: 11.2 us -> 9.19 us  [step(): lax.all_to_all(speeds, ('gx', 'gy'), split_axis=0, concat_axis=0, tiled=T...]
    pallas_call x1 -> x2, Pallas kernels: 4.33 us -> 4.11 us  [the longest x1 3.23 us: step(): pl.pallas_call(functools.partial(place_kernel, capacity), out_shape=(shap...]
  transfers between devices with their start and end apart: 5 -> 5, of which waited for: 4 -> 3; matrix products, arithmetic and copies ran while one was open for 0% -> 0% of each run, Pallas kernels for 0% -> 7%
where the time goes in v2:
time: 48.1 us; the launch traced here: 47.8 us
  waiting for transfers between devices  14.1 us (29%)
  Pallas kernels  13.1 us (27%)
  starting transfers between devices  10.6 us (22%)
  blocking collectives  9.19 us (19%)
  between operations  0.73 us (2%)
    all_to_all x1, blocking collectives, step(): lax.all_to_all(speeds, ('gx', 'gy'), split_axis=0, concat_axis=0, tiled=T...  9.19 us
    ppermute x2, waiting for transfers between devices, swapped(): second = lax.ppermute(second, axis, outer)  7.42 us
    all_to_all x1, starting transfers between devices, step(): lax.all_to_all(sent, ('gx', 'gy'), split_axis=0, concat_axis=0, tiled=True)  7.09 us
    all_to_all x1, waiting for transfers between devices, step(): lax.all_to_all(sent, ('gx', 'gy'), split_axis=0, concat_axis=0, tiled=True)  6.18 us
    pallas_call x1, Pallas kernels, step(): pl.pallas_call(functools.partial(patch_kernel, capacity, strips), out_sha...  4.65 us
    pallas_call x1, Pallas kernels, step(): pl.pallas_call(functools.partial(place_kernel, capacity), out_shape=(shap...  3.23 us
    pallas_call x1, Pallas kernels, step(): pl.pallas_call(functools.partial(second_kernel, capacity), out_shape=(sha...  2.53 us
    ppermute x2, starting transfers between devices, swapped(): first = lax.ppermute(first, axis, inner)  1.91 us
  transfers between devices with their start and end apart: 5, of which 3 were waited for; matrix products, arithmetic and copies ran while one was open for 0% of the time, Pallas kernels for 7%

profile of v2, /device:TPU:0, one launch (start us, length us, event | category | flops | bytes accessed | tf_op | source)
XLA Modules:
  0.0 47.8 jit_solution(5691868097606067082)
XLA Ops:
  0.6 0.0 copy-start
  0.6 4.6 %patches.1 = (bf16[32,16,128]{2,1,0:T(8,128)(2,1)}, f32[27,4,128]{2,1,0:T(4,128)}, f32[27,4,128]{2,1,0:T(4,128)}) custom-call(s32[1,48]{1,0:T(1,128)} %bitcast.4, s32[3,48]{1,0:T(4,128)} %bitcast.7, bf16[48,64,128]{2,1,0:T(8,128)(2,1)} %weights.1, bf16[3,48,128]{2,1,0:T(8,128)(2,1)} %bitcast.6, f32[19,4,32,128]{3,2,1,0:T(8,128)} %populations.3), custom_call_target="tpu_custom_call" | custom-call | tf_op jit(solution)/shard_map/patches/pallas_call | solution.py:847
  5.3 7.1 %all-to-all-start = ((bf16[32,16,128]{2,1,0:T(8,128)(2,1)}), bf16[32,16,128]{2,1,0:T(8,128)(2,1)S(1)}, u32[]{:S(2)}, u32[]{:S(2)}) async-start(bf16[32,16,128]{2,1,0:T(8,128)(2,1)} %get-tuple-element.16), calls=%async_computation | async-start | bytes 262144 | tf_op jit(solution)/shard_map/all_to_all | solution.py:870
  12.4 1.8 %collective-permute-start = (f32[27,4,128]{2,1,0:T(4,128)}, f32[27,4,128]{2,1,0:T(4,128)S(1)}, u32[]{:S(2)}, u32[]{:S(2)}) collective-permute-start(f32[27,4,128]{2,1,0:T(4,128)} %get-tuple-element.19), channel_id=1, source_target_pairs={{0,1},{1,0},{2,3},{3,2},{4,5},{5,4},{6,7},{7,6},{8,9},{9,8},{10,11... | collective-permute-start | bytes 165896 | tf_op jit(solution)/shard_map/ppermute | solution.py:75
  14.2 0.7 %collective-permute-start.1 = (f32[27,4,128]{2,1,0:T(4,128)}, f32[27,4,128]{2,1,0:T(4,128)S(1)}, u32[]{:S(2)}, u32[]{:S(2)}) collective-permute-start(f32[27,4,128]{2,1,0:T(4,128)} %get-tuple-element.20), channel_id=1, source_target_pairs={{1,2},{2,1},{5,6},{6,5},{9,10},{10,9},{13,14},{14,13},{17,18},{18,... | collective-permute-start | bytes 165896 | tf_op jit(solution)/shard_map/ppermute | solution.py:74
  14.9 6.2 %all-to-all-done.got = bf16[32,16,128]{2,1,0:T(8,128)(2,1)S(1)} async-done(((bf16[32,16,128]{2,1,0:T(8,128)(2,1)}), bf16[32,16,128]{2,1,0:T(8,128)(2,1)S(1)}, u32[]{:S(2)}, u32[]{:S(2)}) %all-to-all-start) | async-done | bytes 131104 | tf_op jit(solution)/shard_map/all_to_all | solution.py:870
  21.1 3.2 %place.1 = (f32[768,128]{1,0:T(8,128)S(1)}, s32[32,128]{1,0:T(8,128)S(1)}) custom-call(bf16[32,16,128]{2,1,0:T(8,128)(2,1)S(1)} %all-to-all-done.got), custom_call_target="tpu_custom_call" | custom-call | tf_op jit(solution)/shard_map/place/pallas_call | solution.py:876
  24.3 0.0 collective-permute-done.rim_a
  24.3 0.0 collective-permute-done.1.rim_b
  24.3 0.0 copy-done
  24.3 0.9 %first.1 = (f32[19,4,48,128]{3,2,1,0:T(8,128)S(1)}, f32[480,128]{1,0:T(8,128)S(1)}, f32[480,128]{1,0:T(8,128)S(1)}, f32[3,4,40,128]{3,2,1,0:T(8,128)S(1)}) custom-call(f32[768,128]{1,0:T(8,128)S(1)} %get-tuple-element.18.placed, f32[19,4,32,128]{3,2,1,0:T(8,128)S(1)} %copy-done, f32[27,4,128]{2,1,0:T(4,128)S(1)} %collective-permute-done.rim_a, ...), custom_call_target="tpu_custom_call" | custom-call | tf_op jit(solution)/shard_map/first/pallas_call | solution.py:892
  25.2 0.1 collective-permute-start.2
  25.3 1.0 %collective-permute-start.3 = (f32[480,128]{1,0:T(8,128)S(1)}, f32[480,128]{1,0:T(8,128)S(1)}, u32[]{:S(2)}, u32[]{:S(2)}) collective-permute-start(f32[480,128]{1,0:T(8,128)S(1)} %get-tuple-element.23), channel_id=1, source_target_pairs={{0,28},{4,8},{8,4},{12,16},{16,12},{20,24},{24,20},{28,0},{1,29},{... | collective-permute-start | bytes 737288 | tf_op jit(solution)/shard_map/ppermute | solution.py:74
  26.3 0.5 %collective-permute-done.2.got_a = f32[480,128]{1,0:T(8,128)S(1)} collective-permute-done((f32[480,128]{1,0:T(8,128)S(1)}, f32[480,128]{1,0:T(8,128)S(1)}, u32[]{:S(2)}, u32[]{:S(2)}) %collective-permute-start.2) | collective-permute-done | bytes 245792 | tf_op jit(solution)/shard_map/ppermute | solution.py:75
  26.8 7.4 %collective-permute-done.3.got_b = f32[480,128]{1,0:T(8,128)S(1)} collective-permute-done((f32[480,128]{1,0:T(8,128)S(1)}, f32[480,128]{1,0:T(8,128)S(1)}, u32[]{:S(2)}, u32[]{:S(2)}) %collective-permute-start.3) | collective-permute-done | bytes 245792 | tf_op jit(solution)/shard_map/ppermute | solution.py:74
  34.2 0.0 copy-start.1
  34.2 0.0 copy-start.2
  34.2 0.0 copy-start.3
  34.2 2.5 %second.1 = (f32[19,4,32,128]{3,2,1,0:T(8,128)}, bf16[32,8,128]{2,1,0:T(8,128)(2,1)S(1)}) custom-call(s32[32,128]{1,0:T(8,128)S(1)} %get-tuple-element.17.items, f32[19,4,48,128]{3,2,1,0:T(8,128)S(1)} %get-tuple-element.21.before, f32[480,128]{1,0:T(8,128)S(1)} %collective-permute-done.2.got_a, f32[480,128]{1,0:T(8,128)S(1)} %collective-permute-done.3.got_b, ...), custom_call_target="tpu_custom_call" | custom-call | tf_op jit(solution)/shard_map/second/pallas_call | solution.py:902
  36.8 9.2 %all_to_all.10.returned = bf16[32,8,128]{2,1,0:T(8,128)(2,1)S(1)} all-to-all(bf16[32,8,128]{2,1,0:T(8,128)(2,1)S(1)} %get-tuple-element.26), channel_id=1, replica_groups=mesh['gx'=8,'gy'=4] {'gx','gy'}, dimensions={0} | all-to-all | bytes 131072 | tf_op jit(solution)/shard_map/all_to_all | solution.py:920
  46.0 0.0 copy-done.1
  46.0 0.0 copy-done.2
  46.0 0.0 copy-done.3
  46.0 1.9 %markers.1 = (f32[3,48,128]{2,1,0:T(8,128)}, f32[3,4]{1,0:T(4,128)}) custom-call(s32[1,48]{1,0:T(1,128)S(1)} %bitcast.5, s32[48]{0:T(128)S(1)} %copy-done.3, bf16[32,8,128]{2,1,0:T(8,128)(2,1)S(1)} %all_to_all.10.returned, bf16[48,64,128]{2,1,0:T(8,128)(2,1)S(1)} %copy-done.1), custom_call_target="tpu_custom_call" | custom-call | tf_op jit(solution)/shard_map/markers/pallas_call | solution.py:921
Async XLA Ops:
  0.6 23.7 %copy-start = (f32[19,4,32,128]{3,2,1,0:T(8,128)S(1)}, f32[19,4,32,128]{3,2,1,0:T(8,128)}, u32[]{:S(2)}) copy-start(f32[19,4,32,128]{3,2,1,0:T(8,128)} %populations.3) | copy-start | bytes 3735556
  5.3 15.8 %all-to-all-start = ((bf16[32,16,128]{2,1,0:T(8,128)(2,1)}), bf16[32,16,128]{2,1,0:T(8,128)(2,1)S(1)}, u32[]{:S(2)}, u32[]{:S(2)}) async-start(bf16[32,16,128]{2,1,0:T(8,128)(2,1)} %get-tuple-element.16), calls=%async_computation | async-start | bytes 262144 | tf_op jit(solution)/shard_map/all_to_all | solution.py:870
  12.4 11.9 %collective-permute-start = (f32[27,4,128]{2,1,0:T(4,128)}, f32[27,4,128]{2,1,0:T(4,128)S(1)}, u32[]{:S(2)}, u32[]{:S(2)}) collective-permute-start(f32[27,4,128]{2,1,0:T(4,128)} %get-tuple-element.19), channel_id=1, source_target_pairs={{0,1},{1,0},{2,3},{3,2},{4,5},{5,4},{6,7},{7,6},{8,9},{9,8},{10,11... | collective-permute-start | bytes 165896 | tf_op jit(solution)/shard_map/ppermute | solution.py:75
  14.2 10.1 %collective-permute-start.1 = (f32[27,4,128]{2,1,0:T(4,128)}, f32[27,4,128]{2,1,0:T(4,128)S(1)}, u32[]{:S(2)}, u32[]{:S(2)}) collective-permute-start(f32[27,4,128]{2,1,0:T(4,128)} %get-tuple-element.20), channel_id=1, source_target_pairs={{1,2},{2,1},{5,6},{6,5},{9,10},{10,9},{13,14},{14,13},{17,18},{18,... | collective-permute-start | bytes 165896 | tf_op jit(solution)/shard_map/ppermute | solution.py:74
  25.2 1.6 %collective-permute-start.2 = (f32[480,128]{1,0:T(8,128)S(1)}, f32[480,128]{1,0:T(8,128)S(1)}, u32[]{:S(2)}, u32[]{:S(2)}) collective-permute-start(f32[480,128]{1,0:T(8,128)S(1)} %get-tuple-element.22), channel_id=1, source_target_pairs={{0,4},{4,0},{8,12},{12,8},{16,20},{20,16},{24,28},{28,24},{1,5},{5... | collective-permute-start | bytes 737288 | tf_op jit(solution)/shard_map/ppermute | solution.py:75
  25.3 8.9 %collective-permute-start.3 = (f32[480,128]{1,0:T(8,128)S(1)}, f32[480,128]{1,0:T(8,128)S(1)}, u32[]{:S(2)}, u32[]{:S(2)}) collective-permute-start(f32[480,128]{1,0:T(8,128)S(1)} %get-tuple-element.23), channel_id=1, source_target_pairs={{0,28},{4,8},{8,4},{12,16},{16,12},{20,24},{24,20},{28,0},{1,29},{... | collective-permute-start | bytes 737288 | tf_op jit(solution)/shard_map/ppermute | solution.py:74
  34.2 11.7 %copy-start.1 = (bf16[48,64,128]{2,1,0:T(8,128)(2,1)S(1)}, bf16[48,64,128]{2,1,0:T(8,128)(2,1)}, u32[]{:S(2)}) copy-start(bf16[48,64,128]{2,1,0:T(8,128)(2,1)} %weights.1) | copy-start | bytes 2359300
  34.2 11.7 %copy-start.2 = (s32[48,1]{0,1:T(1,128)S(1)}, s32[48,1]{0,1:T(1,128)}, u32[]{:S(2)}) copy-start(s32[48,1]{0,1:T(1,128)} %param.9) | copy-start | bytes 580
  34.2 11.7 %copy-start.3 = (s32[48]{0:T(128)S(1)}, s32[48]{0:T(128)}, u32[]{:S(2)}) copy-start(s32[48]{0:T(128)} %swimmer.1) | copy-start | bytes 580

commit v3 on v2

--- a/solution.py
+++ b/solution.py
@@ -18,7 +18,8 @@
 REST_LANE = 48
 DUP_LANE = 96
 WIDE_DUPS = 4
-STEP = 4
+STEP = 8
+DUP_STEP = 4
 
 velocities = np.array(
     [
@@ -141,20 +142,8 @@
         return 0
 
     lax.fori_loop(0, targets, reset, 0, unroll=16)
-    for copy in copies[pieces:]:
-        copy.wait()
     extra = jnp.int32(0)
-    for b in range(held):
-        target = owner[0, b]
-        rank = count[target]
-        count[target] = rank + 1
-        place[b] = target * 4 + rank
-        strip = lax.rem(target, strips)
-        y = base[1, b]
-        north = (y >= strip_cells - 5) & (strip < strips - 1)
-        south = (y <= 1) & (strip > 0)
-        again[extra] = b * 4 + rank
-        extra = extra + jnp.where(north | south, 1, 0)
+    powers = strips & (strips - 1) == 0
     force_copy.wait()
     for k in range(3):
         rows[k] = force[k].astype(jnp.float32)
@@ -165,8 +154,22 @@
             )
         spread[16 * b + 12 : 16 * b + 16, :] = jnp.zeros((4, LANES), jnp.float32)
     for g in range(held // 4):
+        if g == 0:
+            for copy in copies[pieces:]:
+                copy.wait()
         if 4 * g % part_blocks == 0:
             copies[4 * g // part_blocks].wait()
+        for b in range(4 * g, 4 * g + 4):
+            target = owner[0, b]
+            rank = count[target]
+            count[target] = rank + 1
+            place[b] = target * 4 + rank
+            strip = target & (strips - 1) if powers else lax.rem(target, strips)
+            y = base[1, b]
+            north = (y >= strip_cells - 5) & (strip < strips - 1)
+            south = (y <= 1) & (strip > 0)
+            again[extra] = b * 4 + rank
+            extra = extra + jnp.where(north | south, 1, 0)
         out = lax.dot_general(
             spread[64 * g : 64 * g + 64, :].astype(jnp.bfloat16),
             weights[4 * g : 4 * g + 4].reshape(4 * cells, LANES),
@@ -193,34 +196,41 @@
         tile = jnp.where(inside, patches[b], record[target])
         record[target] = labelled(tile, rank, base[1, b], base[2, b])
 
+    for j in range(DUP_STEP - 1):
+        again[extra + j] = -1
+
     def put_again(n, _):
-        item = again[n]
-        b, rank = item >> 2, item & 3
-        y, z = base[1, b], base[2, b]
-        to_south = y <= 1
-        target = owner[0, b] + jnp.where(to_south, -1, 1)
-        half = jnp.where(to_south, 0, 1)
-        q = rank + jnp.where(to_south, capacity, 0)
-        moved = pltpu.roll(patches[b], 8 * ((q + half) & 1), 1)
-        wide = q < WIDE_DUPS
-        low = jnp.where(wide, DUP_LANE + 8 * q, 2 * LANES)
-        tile = jnp.where((lane >= low) & (lane < low + 8) & (sub < 12), moved, record[target])
-        tile = labelled(
-            tile, capacity + q, y + jnp.where(to_south, strip_cells, -strip_cells), z
-        )
-        if 2 * capacity > WIDE_DUPS:
-            last = tile[12:16, :]
-            lane4 = lane_iota(4)
-            for k in range(3):
-                low = jnp.where(wide, 2 * LANES, GROUP * k + 8 * (q - WIDE_DUPS))
-                last = jnp.where(
-                    (lane4 >= low) & (lane4 < low + 8), moved[4 * k : 4 * k + 4, :], last
-                )
-            tile = jnp.concatenate([tile[0:12, :], last], axis=0)
-        record[target] = tile
+        todo = []
+        for j in range(DUP_STEP):
+            item = again[DUP_STEP * n + j]
+            none = item < 0
+            b, rank = jnp.where(none, 0, item >> 2), item & 3
+            y, z = base[1, b], base[2, b]
+            to_south = y <= 1
+            target = jnp.where(none, targets, owner[0, b] + jnp.where(to_south, -1, 1))
+            half = jnp.where(to_south, 0, 1)
+            q = rank + jnp.where(to_south, capacity, 0)
+            moved = pltpu.roll(patches[b], 8 * ((q + half) & 1), 1)
+            frame_y = y + jnp.where(to_south, strip_cells, -strip_cells)
+            todo.append((target, q, moved, frame_y, z))
+        for target, q, moved, frame_y, z in todo:
+            wide = q < WIDE_DUPS
+            low = jnp.where(wide, DUP_LANE + 8 * q, 2 * LANES)
+            tile = jnp.where((lane >= low) & (lane < low + 8) & (sub < 12), moved, record[target])
+            tile = labelled(tile, capacity + q, frame_y, z)
+            if 2 * capacity > WIDE_DUPS:
+                last = tile[12:16, :]
+                lane4 = lane_iota(4)
+                for k in range(3):
+                    low = jnp.where(wide, 2 * LANES, GROUP * k + 8 * (q - WIDE_DUPS))
+                    last = jnp.where(
+                        (lane4 >= low) & (lane4 < low + 8), moved[4 * k : 4 * k + 4, :], last
+                    )
+                tile = jnp.concatenate([tile[0:12, :], last], axis=0)
+            record[target] = tile
         return 0
 
-    lax.fori_loop(0, extra, put_again, 0)
+    lax.fori_loop(0, (extra + DUP_STEP - 1) // DUP_STEP, put_again, 0)
     for copy in edge_copies:
         copy.wait()
     write_rims(bottom, top, rim_a, rim_b)
@@ -568,6 +578,8 @@
     for j in range(STEP - 1):
         at = own_count + j
         listing[at >> 7, at & 127] = sources * 4 * 8192 + nowhere
+    for j in range(DUP_STEP - 1):
+        spare[dup_count + j] = sources * 8 * 8192 + nowhere
 
     def moved_rows(source, z, lanes_at, steps):
         inside = (lane >= z) & (lane < z + STEN)
@@ -603,16 +615,20 @@
     lax.fori_loop(0, (own_count + STEP - 1) // STEP, place_own, 0)
 
     def place_dup(n, _):
-        item = spare[n]
-        slot, code = item >> 13, item & 8191
-        q = slot & 7
-        low = jnp.where(q < capacity, 2, 0)
-        at = 8 * q + jnp.where(q < WIDE_DUPS, DUP_LANE, REST_LANE - 8 * WIDE_DUPS)
-        rows = moved_rows(slot >> 3, code & (LANES - 1), at, 2)
-        add_rows(rows, (code >> 7) + low)
+        todo = []
+        for j in range(DUP_STEP):
+            item = spare[DUP_STEP * n + j]
+            slot, code = item >> 13, item & 8191
+            q = slot & 7
+            low = jnp.where(q < capacity, 2, 0)
+            at = 8 * q + jnp.where(q < WIDE_DUPS, DUP_LANE, REST_LANE - 8 * WIDE_DUPS)
+            rows = moved_rows(slot >> 3, code & (LANES - 1), at, 2)
+            todo.append((rows, (code >> 7) + low))
+        for rows, y in todo:
+            add_rows(rows, y)
         return 0
 
-    lax.fori_loop(0, dup_count, place_dup, 0)
+    lax.fori_loop(0, (dup_count + DUP_STEP - 1) // DUP_STEP, place_dup, 0)
 
 
 def first_kernel(placed, populations, rim_a, rim_b, relaxed, face_a, face_b, forcing, rim):
@@ -718,7 +734,10 @@
                         total = total + fields[i]
                     elif velocities[i, k] == -1:
                         total = total - fields[i]
-                fluid[pl.ds(SUB * t * 16 + 4 * k + x, SUB, stride=16), :] = total * inverse
+                speed = total * inverse
+                for b in range(4):
+                    moved = speed if b == 0 else pltpu.roll(speed, STEN * b, 1)
+                    fluid[b, pl.ds(SUB * t * 16 + 4 * k + x, SUB, stride=16), :] = moved
         copies.append(
             pltpu.make_async_copy(populations.at[:, x], populations_far.at[:, x], sems.at[x])
         )
@@ -729,15 +748,19 @@
     def pick(s, _):
         corner = [corners[s, r] for r in range(capacity)]
         tile = jnp.zeros((SUB, LANES), jnp.float32)
-        for h in range(2):
-            for r in range(capacity):
-                y, z = (corner[r] >> 7) - SUB, corner[r] & (LANES - 1)
-                for b in range(4):
-                    low = GROUP * (h * capacity + r) + STEN * b
-                    row = pl.multiple_of((y + b) * 16 + SUB * h, SUB)
-                    shift = (low - z + LANES) & (LANES - 1)
-                    moved = pltpu.roll(fluid[pl.ds(row, SUB), :], shift, 1)
-                    tile = jnp.where((lane >= low) & (lane < low + STEN), moved, tile)
+        for r in range(capacity):
+            y, z = (corner[r] >> 7) - SUB, corner[r] & (LANES - 1)
+            beyond = (lane - z) & (LANES - 1)
+            for h in range(2):
+                rows = [
+                    fluid[b, pl.ds(pl.multiple_of((y + b) * 16 + SUB * h, SUB), SUB), :]
+                    for b in range(4)
+                ]
+                low = GROUP * (h * capacity + r)
+                cube = jnp.where(beyond < 2 * STEN, rows[1], jnp.where(beyond < 3 * STEN, rows[2], rows[3]))
+                cube = jnp.where(beyond < STEN, rows[0], cube)
+                moved = pltpu.roll(cube, (low - z + LANES) & (LANES - 1), 1)
+                tile = jnp.where((lane >= low) & (lane < low + GROUP), moved, tile)
         speeds[s] = tile.astype(jnp.bfloat16)
         return 0
 
@@ -859,10 +882,10 @@
             pltpu.VMEM((3, held, LANES), f32),
             pltpu.VMEM((held * 16, LANES), f32),
             pltpu.VMEM((held, 16, LANES), f32),
-            pltpu.VMEM((devices, 16, LANES), f32),
+            pltpu.VMEM((devices + 1, 16, LANES), f32),
             pltpu.SMEM((devices,), jnp.int32),
             pltpu.SMEM((held,), jnp.int32),
-            pltpu.SMEM((held + 1,), jnp.int32),
+            pltpu.SMEM((held + DUP_STEP,), jnp.int32),
             pltpu.SemaphoreType.DMA((9,)),
         ],
         name="patches",
@@ -882,7 +905,7 @@
             pltpu.SMEM((devices, LANES), jnp.int32),
             pltpu.VMEM(((devices + 1) * 16, LANES), f32),
             pltpu.SMEM((SUB, LANES), jnp.int32),
-            pltpu.SMEM((devices * 2 * capacity + 1,), jnp.int32),
+            pltpu.SMEM((devices * 2 * capacity + DUP_STEP,), jnp.int32),
             pltpu.SMEM((devices + 1,), jnp.int32),
             pltpu.SemaphoreType.DMA,
         ],
@@ -911,7 +934,7 @@
         ]
         + rims
         + [
-            pltpu.VMEM((strip_cells * 16, LANES), f32),
+            pltpu.VMEM((4, strip_cells * 16, LANES), f32),
             pltpu.SemaphoreType.DMA((slab_cells + 1,)),
         ],
         compiler_params=small,

time: 48.1 us -> 47.3 us (0.983)
  Pallas kernels: 13.1 us -> 12.2 us
    pallas_call x1, Pallas kernels: 3.23 us -> 2.63 us  [step(): pl.pallas_call(functools.partial(place_kernel, capacity), out_shape=(shap...]
  transfers between devices with their start and end apart: 5 -> 5, of which waited for: 3 -> 3; matrix products, arithmetic and copies ran while one was open for 0% -> 0% of each run, Pallas kernels for 7% -> 6%
where the time goes in v3:
time: 47.3 us; the launch traced here: 47.1 us
  waiting for transfers between devices  14.2 us (30%)
  Pallas kernels  12.2 us (26%)
  starting transfers between devices  10.8 us (23%)
  blocking collectives  9.19 us (19%)
  between operations  0.73 us (2%)
    all_to_all x1, blocking collectives, step(): lax.all_to_all(speeds, ('gx', 'gy'), split_axis=0, concat_axis=0, tiled=T...  9.19 us
    ppermute x2, waiting for transfers between devices, swapped(): second = lax.ppermute(second, axis, outer)  7.5 us
    all_to_all x1, starting transfers between devices, step(): lax.all_to_all(sent, ('gx', 'gy'), split_axis=0, concat_axis=0, tiled=True)  7.2 us
    all_to_all x1, waiting for transfers between devices, step(): lax.all_to_all(sent, ('gx', 'gy'), split_axis=0, concat_axis=0, tiled=True)  6.18 us
    pallas_call x1, Pallas kernels, step(): pl.pallas_call(functools.partial(patch_kernel, capacity, strips), out_sha...  4.21 us
    pallas_call x1, Pallas kernels, step(): pl.pallas_call(functools.partial(second_kernel, capacity), out_shape=(sha...  2.65 us
    pallas_call x1, Pallas kernels, step(): pl.pallas_call(functools.partial(place_kernel, capacity), out_shape=(shap...  2.63 us
    ppermute x2, starting transfers between devices, swapped(): first = lax.ppermute(first, axis, inner)  1.91 us
  transfers between devices with their start and end apart: 5, of which 3 were waited for; matrix products, arithmetic and copies ran while one was open for 0% of the time, Pallas kernels for 6%

profile of v3, /device:TPU:0, one launch (start us, length us, event | category | flops | bytes accessed | tf_op | source)
XLA Modules:
  0.0 47.1 jit_solution(12380457615430619546)
XLA Ops:
  0.6 0.0 copy-start
  0.6 4.2 %patches.1 = (bf16[32,16,128]{2,1,0:T(8,128)(2,1)}, f32[27,4,128]{2,1,0:T(4,128)}, f32[27,4,128]{2,1,0:T(4,128)}) custom-call(s32[1,48]{1,0:T(1,128)} %bitcast.4, s32[3,48]{1,0:T(4,128)} %bitcast.7, bf16[48,64,128]{2,1,0:T(8,128)(2,1)} %weights.1, bf16[3,48,128]{2,1,0:T(8,128)(2,1)} %bitcast.6, f32[19,4,32,128]{3,2,1,0:T(8,128)} %populations.3), custom_call_target="tpu_custom_call" | custom-call | tf_op jit(solution)/shard_map/patches/pallas_call | solution.py:870
  4.9 7.2 %all-to-all-start = ((bf16[32,16,128]{2,1,0:T(8,128)(2,1)}), bf16[32,16,128]{2,1,0:T(8,128)(2,1)S(1)}, u32[]{:S(2)}, u32[]{:S(2)}) async-start(bf16[32,16,128]{2,1,0:T(8,128)(2,1)} %get-tuple-element.16), calls=%async_computation | async-start | bytes 262144 | tf_op jit(solution)/shard_map/all_to_all | solution.py:893
  12.1 1.8 %collective-permute-start = (f32[27,4,128]{2,1,0:T(4,128)}, f32[27,4,128]{2,1,0:T(4,128)S(1)}, u32[]{:S(2)}, u32[]{:S(2)}) collective-permute-start(f32[27,4,128]{2,1,0:T(4,128)} %get-tuple-element.19), channel_id=1, source_target_pairs={{0,1},{1,0},{2,3},{3,2},{4,5},{5,4},{6,7},{7,6},{8,9},{9,8},{10,11... | collective-permute-start | bytes 165896 | tf_op jit(solution)/shard_map/ppermute | solution.py:76
  13.9 0.7 %collective-permute-start.1 = (f32[27,4,128]{2,1,0:T(4,128)}, f32[27,4,128]{2,1,0:T(4,128)S(1)}, u32[]{:S(2)}, u32[]{:S(2)}) collective-permute-start(f32[27,4,128]{2,1,0:T(4,128)} %get-tuple-element.20), channel_id=1, source_target_pairs={{1,2},{2,1},{5,6},{6,5},{9,10},{10,9},{13,14},{14,13},{17,18},{18,... | collective-permute-start | bytes 165896 | tf_op jit(solution)/shard_map/ppermute | solution.py:75
  14.6 6.2 %all-to-all-done.got = bf16[32,16,128]{2,1,0:T(8,128)(2,1)S(1)} async-done(((bf16[32,16,128]{2,1,0:T(8,128)(2,1)}), bf16[32,16,128]{2,1,0:T(8,128)(2,1)S(1)}, u32[]{:S(2)}, u32[]{:S(2)}) %all-to-all-start) | async-done | bytes 131104 | tf_op jit(solution)/shard_map/all_to_all | solution.py:893
  20.7 2.6 %place.1 = (f32[768,128]{1,0:T(8,128)S(1)}, s32[32,128]{1,0:T(8,128)S(1)}) custom-call(bf16[32,16,128]{2,1,0:T(8,128)(2,1)S(1)} %all-to-all-done.got), custom_call_target="tpu_custom_call" | custom-call | tf_op jit(solution)/shard_map/place/pallas_call | solution.py:899
  23.4 0.0 collective-permute-done.rim_a
  23.4 0.0 collective-permute-done.1.rim_b
  23.4 0.0 copy-done
  23.4 0.9 %first.1 = (f32[19,4,48,128]{3,2,1,0:T(8,128)S(1)}, f32[480,128]{1,0:T(8,128)S(1)}, f32[480,128]{1,0:T(8,128)S(1)}, f32[3,4,40,128]{3,2,1,0:T(8,128)S(1)}) custom-call(f32[768,128]{1,0:T(8,128)S(1)} %get-tuple-element.18.placed, f32[19,4,32,128]{3,2,1,0:T(8,128)S(1)} %copy-done, f32[27,4,128]{2,1,0:T(4,128)S(1)} %collective-permute-done.rim_a, ...), custom_call_target="tpu_custom_call" | custom-call | tf_op jit(solution)/shard_map/first/pallas_call | solution.py:915
  24.3 0.1 collective-permute-start.2
  24.4 1.0 %collective-permute-start.3 = (f32[480,128]{1,0:T(8,128)S(1)}, f32[480,128]{1,0:T(8,128)S(1)}, u32[]{:S(2)}, u32[]{:S(2)}) collective-permute-start(f32[480,128]{1,0:T(8,128)S(1)} %get-tuple-element.23), channel_id=1, source_target_pairs={{0,28},{4,8},{8,4},{12,16},{16,12},{20,24},{24,20},{28,0},{1,29},{... | collective-permute-start | bytes 737288 | tf_op jit(solution)/shard_map/ppermute | solution.py:75
  25.4 0.5 collective-permute-done.2.got_a
  25.9 7.5 %collective-permute-done.3.got_b = f32[480,128]{1,0:T(8,128)S(1)} collective-permute-done((f32[480,128]{1,0:T(8,128)S(1)}, f32[480,128]{1,0:T(8,128)S(1)}, u32[]{:S(2)}, u32[]{:S(2)}) %collective-permute-start.3) | collective-permute-done | bytes 245792 | tf_op jit(solution)/shard_map/ppermute | solution.py:75
  33.4 0.0 copy-start.1
  33.4 0.0 copy-start.2
  33.4 0.0 copy-start.3
  33.4 2.6 %second.1 = (f32[19,4,32,128]{3,2,1,0:T(8,128)}, bf16[32,8,128]{2,1,0:T(8,128)(2,1)S(1)}) custom-call(s32[32,128]{1,0:T(8,128)S(1)} %get-tuple-element.17.items, f32[19,4,48,128]{3,2,1,0:T(8,128)S(1)} %get-tuple-element.21.before, f32[480,128]{1,0:T(8,128)S(1)} %collective-permute-done.2.got_a, f32[480,128]{1,0:T(8,128)S(1)} %collective-permute-done.3.got_b, ...), custom_call_target="tpu_custom_call" | custom-call | tf_op jit(solution)/shard_map/second/pallas_call | solution.py:925
  36.0 9.2 %all_to_all.10.returned = bf16[32,8,128]{2,1,0:T(8,128)(2,1)S(1)} all-to-all(bf16[32,8,128]{2,1,0:T(8,128)(2,1)S(1)} %get-tuple-element.26), channel_id=1, replica_groups=mesh['gx'=8,'gy'=4] {'gx','gy'}, dimensions={0} | all-to-all | bytes 131072 | tf_op jit(solution)/shard_map/all_to_all | solution.py:943
  45.2 0.0 copy-done.1
  45.2 0.0 copy-done.2
  45.2 0.0 copy-done.3
  45.2 1.9 %markers.1 = (f32[3,48,128]{2,1,0:T(8,128)}, f32[3,4]{1,0:T(4,128)}) custom-call(s32[1,48]{1,0:T(1,128)S(1)} %bitcast.5, s32[48]{0:T(128)S(1)} %copy-done.3, bf16[32,8,128]{2,1,0:T(8,128)(2,1)S(1)} %all_to_all.10.returned, bf16[48,64,128]{2,1,0:T(8,128)(2,1)S(1)} %copy-done.1), custom_call_target="tpu_custom_call" | custom-call | tf_op jit(solution)/shard_map/markers/pallas_call | solution.py:944
Async XLA Ops:
  0.6 22.8 %copy-start = (f32[19,4,32,128]{3,2,1,0:T(8,128)S(1)}, f32[19,4,32,128]{3,2,1,0:T(8,128)}, u32[]{:S(2)}) copy-start(f32[19,4,32,128]{3,2,1,0:T(8,128)} %populations.3) | copy-start | bytes 3735556
  4.9 15.9 %all-to-all-start = ((bf16[32,16,128]{2,1,0:T(8,128)(2,1)}), bf16[32,16,128]{2,1,0:T(8,128)(2,1)S(1)}, u32[]{:S(2)}, u32[]{:S(2)}) async-start(bf16[32,16,128]{2,1,0:T(8,128)(2,1)} %get-tuple-element.16), calls=%async_computation | async-start | bytes 262144 | tf_op jit(solution)/shard_map/all_to_all | solution.py:893
  12.1 11.3 %collective-permute-start = (f32[27,4,128]{2,1,0:T(4,128)}, f32[27,4,128]{2,1,0:T(4,128)S(1)}, u32[]{:S(2)}, u32[]{:S(2)}) collective-permute-start(f32[27,4,128]{2,1,0:T(4,128)} %get-tuple-element.19), channel_id=1, source_target_pairs={{0,1},{1,0},{2,3},{3,2},{4,5},{5,4},{6,7},{7,6},{8,9},{9,8},{10,11... | collective-permute-start | bytes 165896 | tf_op jit(solution)/shard_map/ppermute | solution.py:76
  13.9 9.5 %collective-permute-start.1 = (f32[27,4,128]{2,1,0:T(4,128)}, f32[27,4,128]{2,1,0:T(4,128)S(1)}, u32[]{:S(2)}, u32[]{:S(2)}) collective-permute-start(f32[27,4,128]{2,1,0:T(4,128)} %get-tuple-element.20), channel_id=1, source_target_pairs={{1,2},{2,1},{5,6},{6,5},{9,10},{10,9},{13,14},{14,13},{17,18},{18,... | collective-permute-start | bytes 165896 | tf_op jit(solution)/shard_map/ppermute | solution.py:75
  24.3 1.6 %collective-permute-start.2 = (f32[480,128]{1,0:T(8,128)S(1)}, f32[480,128]{1,0:T(8,128)S(1)}, u32[]{:S(2)}, u32[]{:S(2)}) collective-permute-start(f32[480,128]{1,0:T(8,128)S(1)} %get-tuple-element.22), channel_id=1, source_target_pairs={{0,4},{4,0},{8,12},{12,8},{16,20},{20,16},{24,28},{28,24},{1,5},{5... | collective-permute-start | bytes 737288 | tf_op jit(solution)/shard_map/ppermute | solution.py:76
  24.4 9.0 %collective-permute-start.3 = (f32[480,128]{1,0:T(8,128)S(1)}, f32[480,128]{1,0:T(8,128)S(1)}, u32[]{:S(2)}, u32[]{:S(2)}) collective-permute-start(f32[480,128]{1,0:T(8,128)S(1)} %get-tuple-element.23), channel_id=1, source_target_pairs={{0,28},{4,8},{8,4},{12,16},{16,12},{20,24},{24,20},{28,0},{1,29},{... | collective-permute-start | bytes 737288 | tf_op jit(solution)/shard_map/ppermute | solution.py:75
  33.4 11.9 %copy-start.1 = (bf16[48,64,128]{2,1,0:T(8,128)(2,1)S(1)}, bf16[48,64,128]{2,1,0:T(8,128)(2,1)}, u32[]{:S(2)}) copy-start(bf16[48,64,128]{2,1,0:T(8,128)(2,1)} %weights.1) | copy-start | bytes 2359300
  33.4 11.9 %copy-start.2 = (s32[48,1]{0,1:T(1,128)S(1)}, s32[48,1]{0,1:T(1,128)}, u32[]{:S(2)}) copy-start(s32[48,1]{0,1:T(1,128)} %param.9) | copy-start | bytes 580
  33.4 11.9 %copy-start.3 = (s32[48]{0:T(128)S(1)}, s32[48]{0:T(128)}, u32[]{:S(2)}) copy-start(s32[48]{0:T(128)} %swimmer.1) | copy-start | bytes 580

commit v4 on v3

--- a/solution.py
+++ b/solution.py
@@ -695,30 +695,37 @@
     unpack_faces(got_a, got_b, tiles, rim_west, rim_east)
     walls = wall_flags()
     rims = (rim_west, rim_east)
-    relax_rim(
-        before, rims, slabs, tiles, walls, got_a, got_b, going_east, going_west, -1, True, after_west
-    )
-    relax_rim(
-        before,
-        rims,
-        slabs,
-        tiles,
-        walls,
-        got_a,
-        got_b,
-        going_west,
-        going_east,
-        slabs,
-        False,
-        after_east,
-    )
-    for x in range(slabs):
+
+    def relax_side(is_west):
+        relax_rim(
+            before,
+            rims,
+            slabs,
+            tiles,
+            walls,
+            got_a,
+            got_b,
+            going_east if is_west else going_west,
+            going_west if is_west else going_east,
+            -1 if is_west else slabs,
+            is_west,
+            after_west if is_west else after_east,
+        )
+
+    def relax_plane(x):
         for t in range(tiles + 1):
             fields = streamed(before, rim_west, rim_east, slabs, tiles, x, t, walls)
             push = [forcing[k, x, SUB * t : SUB * t + SUB, :] for k in range(3)]
             keep_tile(relaxed, tiles, x, t, collided(fields, push))
+
+    relax_side(True)
+    relax_plane(0)
     copies = []
     for x in range(slabs):
+        if x + 1 < slabs:
+            relax_plane(x + 1)
+        else:
+            relax_side(False)
         for t in range(tiles):
             fields = streamed(relaxed, after_west, after_east, slabs, tiles, x, t, walls)
             density = fields[0]

time: 47.3 us -> 47.1 us (level)
  no operation moved by 1% of the time
where the time goes in v4:
time: 47.1 us; the launch traced here: 46.9 us
  waiting for transfers between devices  14.2 us (30%)
  Pallas kernels  12 us (25%)
  starting transfers between devices  10.8 us (23%)
  blocking collectives  9.19 us (20%)
  between operations  0.73 us (2%)
    all_to_all x1, blocking collectives, step(): lax.all_to_all(speeds, ('gx', 'gy'), split_axis=0, concat_axis=0, tiled=T...  9.19 us
    ppermute x2, waiting for transfers between devices, swapped(): second = lax.ppermute(second, axis, outer)  7.5 us
    all_to_all x1, starting transfers between devices, step(): lax.all_to_all(sent, ('gx', 'gy'), split_axis=0, concat_axis=0, tiled=True)  7.2 us
    all_to_all x1, waiting for transfers between devices, step(): lax.all_to_all(sent, ('gx', 'gy'), split_axis=0, concat_axis=0, tiled=True)  6.18 us
    pallas_call x1, Pallas kernels, step(): pl.pallas_call(functools.partial(patch_kernel, capacity, strips), out_sha...  4.21 us
    pallas_call x1, Pallas kernels, step(): pl.pallas_call(functools.partial(place_kernel, capacity), out_shape=(shap...  2.63 us
    pallas_call x1, Pallas kernels, step(): pl.pallas_call(functools.partial(second_kernel, capacity), out_shape=(sha...  2.41 us
    ppermute x2, starting transfers between devices, swapped(): first = lax.ppermute(first, axis, inner)  1.91 us
  transfers between devices with their start and end apart: 5, of which 3 were waited for; matrix products, arithmetic and copies ran while one was open for 0% of the time, Pallas kernels for 6%

profile of v4, /device:TPU:0, one launch (start us, length us, event | category | flops | bytes accessed | tf_op | source)
XLA Modules:
  0.0 46.9 jit_solution(628604904746303156)
XLA Ops:
  0.6 0.0 copy-start
  0.6 4.2 %patches.1 = (bf16[32,16,128]{2,1,0:T(8,128)(2,1)}, f32[27,4,128]{2,1,0:T(4,128)}, f32[27,4,128]{2,1,0:T(4,128)}) custom-call(s32[1,48]{1,0:T(1,128)} %bitcast.4, s32[3,48]{1,0:T(4,128)} %bitcast.7, bf16[48,64,128]{2,1,0:T(8,128)(2,1)} %weights.1, bf16[3,48,128]{2,1,0:T(8,128)(2,1)} %bitcast.6, f32[19,4,32,128]{3,2,1,0:T(8,128)} %populations.3), custom_call_target="tpu_custom_call" | custom-call | tf_op jit(solution)/shard_map/patches/pallas_call | solution.py:877
  4.9 7.2 %all-to-all-start = ((bf16[32,16,128]{2,1,0:T(8,128)(2,1)}), bf16[32,16,128]{2,1,0:T(8,128)(2,1)S(1)}, u32[]{:S(2)}, u32[]{:S(2)}) async-start(bf16[32,16,128]{2,1,0:T(8,128)(2,1)} %get-tuple-element.16), calls=%async_computation | async-start | bytes 262144 | tf_op jit(solution)/shard_map/all_to_all | solution.py:900
  12.1 1.8 %collective-permute-start = (f32[27,4,128]{2,1,0:T(4,128)}, f32[27,4,128]{2,1,0:T(4,128)S(1)}, u32[]{:S(2)}, u32[]{:S(2)}) collective-permute-start(f32[27,4,128]{2,1,0:T(4,128)} %get-tuple-element.19), channel_id=1, source_target_pairs={{0,1},{1,0},{2,3},{3,2},{4,5},{5,4},{6,7},{7,6},{8,9},{9,8},{10,11... | collective-permute-start | bytes 165896 | tf_op jit(solution)/shard_map/ppermute | solution.py:76
  13.9 0.7 %collective-permute-start.1 = (f32[27,4,128]{2,1,0:T(4,128)}, f32[27,4,128]{2,1,0:T(4,128)S(1)}, u32[]{:S(2)}, u32[]{:S(2)}) collective-permute-start(f32[27,4,128]{2,1,0:T(4,128)} %get-tuple-element.20), channel_id=1, source_target_pairs={{1,2},{2,1},{5,6},{6,5},{9,10},{10,9},{13,14},{14,13},{17,18},{18,... | collective-permute-start | bytes 165896 | tf_op jit(solution)/shard_map/ppermute | solution.py:75
  14.6 6.2 %all-to-all-done.got = bf16[32,16,128]{2,1,0:T(8,128)(2,1)S(1)} async-done(((bf16[32,16,128]{2,1,0:T(8,128)(2,1)}), bf16[32,16,128]{2,1,0:T(8,128)(2,1)S(1)}, u32[]{:S(2)}, u32[]{:S(2)}) %all-to-all-start) | async-done | bytes 131104 | tf_op jit(solution)/shard_map/all_to_all | solution.py:900
  20.7 2.6 %place.1 = (f32[768,128]{1,0:T(8,128)S(1)}, s32[32,128]{1,0:T(8,128)S(1)}) custom-call(bf16[32,16,128]{2,1,0:T(8,128)(2,1)S(1)} %all-to-all-done.got), custom_call_target="tpu_custom_call" | custom-call | tf_op jit(solution)/shard_map/place/pallas_call | solution.py:906
  23.4 0.0 collective-permute-done.rim_a
  23.4 0.0 collective-permute-done.1.rim_b
  23.4 0.0 copy-done
  23.4 0.9 %first.1 = (f32[19,4,48,128]{3,2,1,0:T(8,128)S(1)}, f32[480,128]{1,0:T(8,128)S(1)}, f32[480,128]{1,0:T(8,128)S(1)}, f32[3,4,40,128]{3,2,1,0:T(8,128)S(1)}) custom-call(f32[768,128]{1,0:T(8,128)S(1)} %get-tuple-element.18.placed, f32[19,4,32,128]{3,2,1,0:T(8,128)S(1)} %copy-done, f32[27,4,128]{2,1,0:T(4,128)S(1)} %collective-permute-done.rim_a, ...), custom_call_target="tpu_custom_call" | custom-call | tf_op jit(solution)/shard_map/first/pallas_call | solution.py:922
  24.3 0.1 collective-permute-start.2
  24.4 1.0 %collective-permute-start.3 = (f32[480,128]{1,0:T(8,128)S(1)}, f32[480,128]{1,0:T(8,128)S(1)}, u32[]{:S(2)}, u32[]{:S(2)}) collective-permute-start(f32[480,128]{1,0:T(8,128)S(1)} %get-tuple-element.23), channel_id=1, source_target_pairs={{0,28},{4,8},{8,4},{12,16},{16,12},{20,24},{24,20},{28,0},{1,29},{... | collective-permute-start | bytes 737288 | tf_op jit(solution)/shard_map/ppermute | solution.py:75
  25.4 0.5 collective-permute-done.2.got_a
  25.9 7.5 %collective-permute-done.3.got_b = f32[480,128]{1,0:T(8,128)S(1)} collective-permute-done((f32[480,128]{1,0:T(8,128)S(1)}, f32[480,128]{1,0:T(8,128)S(1)}, u32[]{:S(2)}, u32[]{:S(2)}) %collective-permute-start.3) | collective-permute-done | bytes 245792 | tf_op jit(solution)/shard_map/ppermute | solution.py:75
  33.4 0.0 copy-start.1
  33.4 0.0 copy-start.2
  33.4 0.0 copy-start.3
  33.4 2.4 %second.1 = (f32[19,4,32,128]{3,2,1,0:T(8,128)}, bf16[32,8,128]{2,1,0:T(8,128)(2,1)S(1)}) custom-call(s32[32,128]{1,0:T(8,128)S(1)} %get-tuple-element.17.items, f32[19,4,48,128]{3,2,1,0:T(8,128)S(1)} %get-tuple-element.21.before, f32[480,128]{1,0:T(8,128)S(1)} %collective-permute-done.2.got_a, f32[480,128]{1,0:T(8,128)S(1)} %collective-permute-done.3.got_b, ...), custom_call_target="tpu_custom_call" | custom-call | tf_op jit(solution)/shard_map/second/pallas_call | solution.py:932
  35.8 9.2 %all_to_all.10.returned = bf16[32,8,128]{2,1,0:T(8,128)(2,1)S(1)} all-to-all(bf16[32,8,128]{2,1,0:T(8,128)(2,1)S(1)} %get-tuple-element.26), channel_id=1, replica_groups=mesh['gx'=8,'gy'=4] {'gx','gy'}, dimensions={0} | all-to-all | bytes 131072 | tf_op jit(solution)/shard_map/all_to_all | solution.py:950
  45.0 0.0 copy-done.1
  45.0 0.0 copy-done.2
  45.0 0.0 copy-done.3
  45.0 1.9 %markers.1 = (f32[3,48,128]{2,1,0:T(8,128)}, f32[3,4]{1,0:T(4,128)}) custom-call(s32[1,48]{1,0:T(1,128)S(1)} %bitcast.5, s32[48]{0:T(128)S(1)} %copy-done.3, bf16[32,8,128]{2,1,0:T(8,128)(2,1)S(1)} %all_to_all.10.returned, bf16[48,64,128]{2,1,0:T(8,128)(2,1)S(1)} %copy-done.1), custom_call_target="tpu_custom_call" | custom-call | tf_op jit(solution)/shard_map/markers/pallas_call | solution.py:951
Async XLA Ops:
  0.6 22.8 %copy-start = (f32[19,4,32,128]{3,2,1,0:T(8,128)S(1)}, f32[19,4,32,128]{3,2,1,0:T(8,128)}, u32[]{:S(2)}) copy-start(f32[19,4,32,128]{3,2,1,0:T(8,128)} %populations.3) | copy-start | bytes 3735556
  4.9 15.9 %all-to-all-start = ((bf16[32,16,128]{2,1,0:T(8,128)(2,1)}), bf16[32,16,128]{2,1,0:T(8,128)(2,1)S(1)}, u32[]{:S(2)}, u32[]{:S(2)}) async-start(bf16[32,16,128]{2,1,0:T(8,128)(2,1)} %get-tuple-element.16), calls=%async_computation | async-start | bytes 262144 | tf_op jit(solution)/shard_map/all_to_all | solution.py:900
  12.1 11.3 %collective-permute-start = (f32[27,4,128]{2,1,0:T(4,128)}, f32[27,4,128]{2,1,0:T(4,128)S(1)}, u32[]{:S(2)}, u32[]{:S(2)}) collective-permute-start(f32[27,4,128]{2,1,0:T(4,128)} %get-tuple-element.19), channel_id=1, source_target_pairs={{0,1},{1,0},{2,3},{3,2},{4,5},{5,4},{6,7},{7,6},{8,9},{9,8},{10,11... | collective-permute-start | bytes 165896 | tf_op jit(solution)/shard_map/ppermute | solution.py:76
  13.9 9.5 %collective-permute-start.1 = (f32[27,4,128]{2,1,0:T(4,128)}, f32[27,4,128]{2,1,0:T(4,128)S(1)}, u32[]{:S(2)}, u32[]{:S(2)}) collective-permute-start(f32[27,4,128]{2,1,0:T(4,128)} %get-tuple-element.20), channel_id=1, source_target_pairs={{1,2},{2,1},{5,6},{6,5},{9,10},{10,9},{13,14},{14,13},{17,18},{18,... | collective-permute-start | bytes 165896 | tf_op jit(solution)/shard_map/ppermute | solution.py:75
  24.3 1.6 %collective-permute-start.2 = (f32[480,128]{1,0:T(8,128)S(1)}, f32[480,128]{1,0:T(8,128)S(1)}, u32[]{:S(2)}, u32[]{:S(2)}) collective-permute-start(f32[480,128]{1,0:T(8,128)S(1)} %get-tuple-element.22), channel_id=1, source_target_pairs={{0,4},{4,0},{8,12},{12,8},{16,20},{20,16},{24,28},{28,24},{1,5},{5... | collective-permute-start | bytes 737288 | tf_op jit(solution)/shard_map/ppermute | solution.py:76
  24.4 9.0 %collective-permute-start.3 = (f32[480,128]{1,0:T(8,128)S(1)}, f32[480,128]{1,0:T(8,128)S(1)}, u32[]{:S(2)}, u32[]{:S(2)}) collective-permute-start(f32[480,128]{1,0:T(8,128)S(1)} %get-tuple-element.23), channel_id=1, source_target_pairs={{0,28},{4,8},{8,4},{12,16},{16,12},{20,24},{24,20},{28,0},{1,29},{... | collective-permute-start | bytes 737288 | tf_op jit(solution)/shard_map/ppermute | solution.py:75
  33.4 11.6 %copy-start.1 = (bf16[48,64,128]{2,1,0:T(8,128)(2,1)S(1)}, bf16[48,64,128]{2,1,0:T(8,128)(2,1)}, u32[]{:S(2)}) copy-start(bf16[48,64,128]{2,1,0:T(8,128)(2,1)} %weights.1) | copy-start | bytes 2359300
  33.4 11.6 %copy-start.2 = (s32[48,1]{0,1:T(1,128)S(1)}, s32[48,1]{0,1:T(1,128)}, u32[]{:S(2)}) copy-start(s32[48,1]{0,1:T(1,128)} %param.9) | copy-start | bytes 580
  33.4 11.6 %copy-start.3 = (s32[48]{0:T(128)S(1)}, s32[48]{0:T(128)}, u32[]{:S(2)}) copy-start(s32[48]{0:T(128)} %swimmer.1) | copy-start | bytes 580
